TPU v7x, 32 devices: a whole 2x2x4 slice. The times are simulated.
32 devices in a mesh: tile: 16 (over z, y, x), day: 2 (over core).
Axes of the slice: x: 2, y: 2, z: 4, core: 2. Of those that a mesh axis runs over, the one named last changes fastest.
Arguments:
- spectra: bfloat16 [2, 4096, 2, 4, 512], P('day', 'tile'), may hold values from -500 to 500
- band_low: int32 [32], P('tile'), may hold values from 0 to 127
- band_high: int32 [32], P('tile'), may hold values from 384 to 512
- pair_list: int32 [64, 2], P('tile'), may hold values from -1 to 31, as said below
Outputs:
- correlations: float32 [2, 64, 128, 128], P('day', 'tile')
Inputs may be any that keep to these rules, and one draw needn't show every extreme that they name: `pair_list`: row p is either a pair (a, b) with 2 * (p // 4) <= a < 2 * (p // 4) + 2 and 0 <= b - a <= 6, or (-1, -1). In each aligned run of 4 rows the pairs come first, there is at least one, and in every draw some run holds 4 pairs.
All inputs are finite; a program needn't handle non-finite values.
Results may differ from a plain program's by a relative error of at most 0.0027.
Values may be sent and summed in bfloat16 or wider, within the bound.
A program may use at most 128 MiB of HBM per device.

v0:
```python
import math

import jax
import jax.numpy as jnp
from jax import lax
from jax.sharding import PartitionSpec as P

BLK_DEV = 2
SEGLEN = 15000
FIRST = 90
HALF_WIN = 64
LAG_DEV = 1
LSTEP = 25
REACH = 3


def shifted(x, axis, by):
    count = lax.axis_size(axis)
    pairs = [(i, i + by) for i in range(count) if 0 <= i + by < count]
    return lax.ppermute(x, axis, pairs)


def spread_mean(magnitude, bin_count):
    prefix = jnp.cumsum(magnitude, axis=-1, dtype=jnp.float32)
    lead_shape = magnitude.shape[:-1]
    zero_col = jnp.zeros(lead_shape + (1,), jnp.float32)
    prefix = jnp.concatenate([zero_col, prefix], axis=-1)
    last_col = prefix[..., bin_count:]
    upper = jnp.concatenate(
        [
            prefix[..., HALF_WIN + 1 :],
            jnp.broadcast_to(last_col, lead_shape + (min(HALF_WIN, bin_count),)),
        ],
        axis=-1,
    )
    lower = jnp.concatenate(
        [jnp.zeros(lead_shape + (HALF_WIN,), jnp.float32), prefix[..., :bin_count]], axis=-1
    )[..., :bin_count]
    bin_index = jnp.arange(bin_count, dtype=jnp.int32)
    bin_counts = (
        jnp.minimum(bin_index + HALF_WIN, bin_count - 1) - jnp.maximum(bin_index - HALF_WIN, 0) + 1
    ).astype(jnp.float32)
    return (upper - lower) / bin_counts + 1e-05


def whiten(raw):
    values = raw.astype(jnp.float32)
    magnitude = jnp.sqrt(values[:, 0] * values[:, 0] + values[:, 1] * values[:, 1])
    amplitude = spread_mean(magnitude, raw.shape[-1])
    return (values / amplitude[:, None]).astype(jnp.bfloat16)


def phase_tables(lag_total, all_lags, bin_count):
    lag_index = jnp.arange(lag_total, dtype=jnp.int32)
    lag_samples = (lag_index - all_lags // 2) * LSTEP
    bin_number = FIRST + jnp.arange(bin_count, dtype=jnp.int32)
    phase_turns = lag_samples[:, None] * bin_number[None, :] % SEGLEN
    phase_angle = phase_turns.astype(jnp.float32) * (2.0 * math.pi / SEGLEN)
    return (jnp.cos(phase_angle), jnp.sin(phase_angle))


def rotate(partner, cos_joint, sin_joint):
    values = partner.astype(jnp.float32)
    real_part = values[None, :, 0]
    imag_part = values[None, :, 1]
    cosine = cos_joint[:, None, None, :]
    sine_part = sin_joint[:, None, None, :]
    rotated = jnp.stack(
        [real_part * cosine + imag_part * sine_part, imag_part * cosine - real_part * sine_part],
        axis=2,
    )
    return rotated.astype(jnp.bfloat16)


def per_device(spectra, band_low, band_high, pair_list):
    tile_here = lax.axis_index("tile")
    day_count = lax.axis_size("day")
    total_lags = LAG_DEV * day_count
    own_blocks = spectra[0]
    bin_count = own_blocks.shape[-1]
    segments = own_blocks.shape[2]
    block_rows = own_blocks.shape[0] // BLK_DEV
    bin_index = jnp.arange(bin_count, dtype=jnp.int32)
    keep_mask = (
        (bin_index[None, :] >= band_low[:, None]) & (bin_index[None, :] < band_high[:, None])
    ).astype(jnp.bfloat16)
    payload = whiten(own_blocks)
    window = payload
    window_keep = keep_mask
    for section in range(REACH.bit_length()):
        arrived, arrived_keep = shifted((window, window_keep), "tile", -(1 << section))
        window = jnp.concatenate([window, arrived], axis=0)
        window_keep = jnp.concatenate([window_keep, arrived_keep], axis=0)
    stacked = window.reshape(-1, block_rows, 2, segments, bin_count)
    live_rows = jnp.sum((pair_list[:, 0] >= 0).astype(jnp.int32))
    norm_factor = 1.0 / math.sqrt(segments * bin_count * day_count)
    row_count = LAG_DEV * lax.axis_size("day")
    cosine, sine_part = phase_tables(row_count, total_lags, bin_count)

    def add_pair(slot_index, totals):
        first_block = pair_list[slot_index, 0] - BLK_DEV * tile_here
        second_block = pair_list[slot_index, 1] - BLK_DEV * tile_here
        left_block = lax.dynamic_index_in_dim(stacked, first_block, 0, keepdims=False)
        partner = lax.dynamic_index_in_dim(stacked, second_block, 0, keepdims=False)
        first_keep = lax.dynamic_index_in_dim(window_keep, first_block, 0, keepdims=False).astype(
            jnp.float32
        )
        second_keep = lax.dynamic_index_in_dim(window_keep, second_block, 0, keepdims=False).astype(
            jnp.float32
        )
        joint_keep = first_keep * second_keep
        rotated = rotate(partner, cosine * joint_keep, sine_part * joint_keep)
        left_flat = left_block.reshape(block_rows, -1)
        rotated_flat = rotated.reshape(row_count * block_rows, -1)
        product = lax.dot_general(
            left_flat, rotated_flat, (((1,), (1,)), ((), ())), preferred_element_type=jnp.float32
        )
        product = (
            jnp.transpose(product.reshape(block_rows, row_count, block_rows), (1, 0, 2))
            * norm_factor
        )
        return lax.dynamic_update_slice(totals, product[:, None], (0, slot_index, 0, 0))

    initial = jnp.zeros((row_count, pair_list.shape[0], block_rows, block_rows), jnp.float32)
    return lax.psum_scatter(
        lax.fori_loop(0, live_rows, add_pair, initial), "day", scatter_dimension=0, tiled=True
    )


def solution(mesh):
    placed = (P("day", "tile", None, None, None), P("tile"), P("tile"), P("tile", None))
    return jax.shard_map(
        per_device,
        mesh=mesh,
        in_specs=placed,
        out_specs=P("day", "tile", None, None),
        check_vma=False,
    )
```

profile of v0, /device:TPU:0, one launch (start us, length us, event | category | flops | bytes accessed | tf_op | source)
XLA Modules:
  0.0 276.0 jit_solution(3891796097017397884)
XLA Ops:
  6.5 0.0 reduce-scatter.2.cloned.1.call-start
  6.5 2.8 %bitcast_convert_fusion.1 = f32[256,2,4,512]{3,2,1,0:T(4,128)S(1)} fusion(bf16[1,256,2,4,512]{4,3,2,1,0:T(4,128)(2,1)} %param.6), kind=kLoop, calls=%fused_computation.32 | loop fusion | flops 1048576 | bytes 6291456 | tf_op jit(solution)/shard_map/convert_element_type | solution.py:47
  9.4 1.4 fusion.12
  10.7 2.3 sqrt.8
  13.0 4.2 %copy.7 = f32[256,4,4,128]{0,2,1,3:T(4,128)} copy(f32[256,4,4,128]{3,2,1,0:T(4,128)} %sqrt.8) | data formatting | bytes 4194304 | tf_op jit(solution)/shard_map/sqrt | solution.py:48
  17.2 2.0 fusion.19
  19.2 0.2 broadcast_add_fusion
  19.4 1.2 copy.8
  20.6 0.1 pad_slice_fusion.1
  20.8 0.1 slice.58
  21.0 0.4 fusion.10
  21.4 2.0 copy.9
  23.4 3.4 %divide_convert_fusion = bf16[256,2,4,512]{3,2,1,0:T(4,128)(2,1)S(1)} fusion(f32[256,4,512]{2,1,0:T(4,128)} %copy.9, bf16[1,256,2,4,512]{4,3,2,1,0:T(4,128)(2,1)} %param.6), kind=kLoop, calls=%fused_computation.22 | loop fusion | flops 3145728 | bytes 6291456 | tf_op jit(solution)/shard_map/convert_element_type | solution.py:50
  26.8 0.0 copy-start.2
  26.8 0.0 copy-start.3
  26.8 0.0 copy-start.1
  26.8 1.4 collective-permute-start
  28.2 49.2 %collective-permute-done = bf16[256,2,4,512]{3,2,1,0:T(4,128)(2,1)S(1)} collective-permute-done((bf16[256,2,4,512]{3,2,1,0:T(4,128)(2,1)S(1)}, bf16[256,2,4,512]{3,2,1,0:T(4,128)(2,1)S(1)}, u32[]{:S(2)}, u32[]{:S(2)}) %collective-permute-start) | collective-permute-done | bytes 2097184 | tf_op jit(solution)/shard_map/ppermute | solution.py:20
  77.4 0.0 copy-start
  77.4 4.6 %pad_maximum_fusion.2 = bf16[512,2,4,512]{3,2,1,0:T(4,128)(2,1)} fusion(bf16[256,2,4,512]{3,2,1,0:T(4,128)(2,1)S(1)} %collective-permute-done, bf16[256,2,4,512]{3,2,1,0:T(4,128)(2,1)S(1)} %divide_convert_fusion), kind=kLoop, calls=%fused_computation.21 | loop fusion | flops 2097152 | bytes 8388608 | tf_op jit(solution)/shard_map/concatenate | solution.py:92
  82.1 0.0 copy-done
  82.1 1.3 collective-permute-start.1
  83.4 0.0 copy-done.2
  83.4 0.0 copy-done.3
  83.4 0.1 and_convert_fusion
  83.5 1.3 collective-permute-start.2
  84.7 0.0 copy-done.1
  84.8 0.7 fusion.18
  85.5 4.1 %collective-permute-done.2 = bf16[2,512]{1,0:T(2,128)(2,1)S(1)} collective-permute-done((bf16[2,512]{1,0:T(2,128)(2,1)S(1)}, bf16[2,512]{1,0:T(2,128)(2,1)S(1)}, u32[]{:S(2)}, u32[]{:S(2)}) %collective-permute-start.2) | collective-permute-done | bytes 2080 | tf_op jit(solution)/shard_map/ppermute | solution.py:20
  89.6 1.5 collective-permute-start.3
  91.0 85.0 %collective-permute-done.3 = bf16[4,512]{1,0:T(4,128)(2,1)S(1)} collective-permute-done((bf16[4,512]{1,0:T(4,128)(2,1)S(1)}, bf16[4,512]{1,0:T(4,128)(2,1)S(1)}, u32[]{:S(2)}, u32[]{:S(2)}) %collective-permute-start.3) | collective-permute-done | bytes 4128 | tf_op jit(solution)/shard_map/ppermute | solution.py:20
  176.1 0.0 collective-permute-done.1
  176.1 8.2 %pad_maximum_fusion.1 = bf16[1024,2,4,512]{3,2,1,0:T(4,128)(2,1)} fusion(bf16[512,2,4,512]{3,2,1,0:T(4,128)(2,1)} %collective-permute-done.1, bf16[256,2,4,512]{3,2,1,0:T(4,128)(2,1)} %copy-done, bf16[256,2,4,512]{3,2,1,0:T(4,128)(2,1)S(1)} %divide_convert_fusion), kind=kLoop, calls=%fused_computation.20 | loop fusion | flops 8388608 | bytes 16777216 | tf_op jit(solution)/shard_map/concatenate | solution.py:92
  184.3 0.8 broadcast_in_dim.10.clone
  185.1 17.6 %while.14 = (s32[]{:T(128)}, f32[2,4,128,128]{3,2,1,0:T(8,128)}, s32[]{:T(128)}, s32[4,2]{0,1:T(2,128)S(1)}, s32[]{:T(128)}, /*index=5*/bf16[8,128,2,4,512]{4,3,...) while((s32[]{:T(128)}, f32[2,4,128,128]{3,2,1,0:T(8,128)}, ...), condition=%wide.region_4.5_spmd.clone.clone, body=%wide.region_3.4_spmd.clone.clone.sunk | while | flops 274248192 | bytes 27418924 | solution.py:126
  185.8 0.7 constant_dynamic-slice_fusion.4
  187.8 3.3 %bitcast_convert_fusion.3 = (f32[128,2,4,512]{3,2,1,0:T(4,128)S(1)}, bf16[1,128,2,4,512]{4,3,2,1,0:T(4,128)(2,1)}) fusion(bf16[8,128,2,4,512]{4,3,2,1,0:T(4,128)(2,1)} %get-tuple-element.305, s32[]{:T(128)S(6)} %select_n.62, s32[]{:T(128)S(6)} %select_n.63), kind=kLoop, calls=%fused_computation.10.clone.1 | loop fusion | flops 524288 | bytes 5242888 | tf_op jit(solution)/shard_map/while/body/convert_element_type | solution.py:63
  191.1 0.4 slice_bitcast_fusion.4
  191.5 0.2 cosine_multiply_fusion.2
  191.7 1.1 add_convert_fusion.2
  192.8 2.7 pad_maximum_fusion.6
  195.5 3.3 %convert_element_type.111 = bf16[2,128,4096]{2,1,0:T(8,128)(2,1)S(1)} reshape(bf16[2,128,2,4,512]{4,3,2,1,0:T(4,128)(2,1)} %pad_maximum_fusion.6) | data formatting | bytes 4194304 | tf_op jit(solution)/shard_map/while/body/convert_element_type | solution.py:72
  198.8 1.8 reshape.134
  200.6 1.5 fusion.28
  202.7 0.0 reduce-scatter.2.cloned.1.call-update
  202.8 66.4 %reduce-scatter.2.cloned.1.call-done = f32[1,4,128,128]{3,2,1,0:T(8,128)} async-done(((f32[2,4,128,128]{3,2,1,0:T(8,128)}), f32[1,4,128,128]{3,2,1,0:T(8,128)}) %reduce-scatter.2.cloned.1.call-update) | async-done | bytes 262160 | tf_op jit(solution)/shard_map/reduce_scatter | solution.py:125
  (12 shorter events, 0.1 us)
Async XLA Ops:
  6.5 262.6 %reduce-scatter.2.cloned.1.call-start = ((), (), s32[]{:S(2)}) async-start(), calls=%async_computation.1 | async-start | bytes 786432 | tf_op jit(solution)/shard_map/reduce_scatter | solution.py:125
  26.8 56.6 %copy-start.2 = (s32[2]{0:T(128)S(1)}, s32[2]{0:T(128)}, u32[]{:S(2)}) copy-start(s32[2]{0:T(128)} %param.8) | copy-start | bytes 28
  26.8 56.6 %copy-start.3 = (s32[2]{0:T(128)S(1)}, s32[2]{0:T(128)}, u32[]{:S(2)}) copy-start(s32[2]{0:T(128)} %param.7) | copy-start | bytes 28
  26.8 58.0 %copy-start.1 = (s32[4,2]{0,1:T(2,128)S(1)}, s32[4,2]{0,1:T(2,128)}, u32[]{:S(2)}) copy-start(s32[4,2]{0,1:T(2,128)} %param.9) | copy-start | bytes 100
  26.8 50.6 %collective-permute-start = (bf16[256,2,4,512]{3,2,1,0:T(4,128)(2,1)S(1)}, bf16[256,2,4,512]{3,2,1,0:T(4,128)(2,1)S(1)}, u32[]{:S(2)}, u32[]{:S(2)}) collective-permute-start(bf16[256,2,4,512]{3,2,1,0:T(4,128)(2,1)S(1)} %divide_convert_fusion), channel_id=1, source_target_pairs={{2,0},{4,2},{6,4},{8,6},{10,8},{12,10},{14,12},{16,14},{18,16},{20... | collective-permute-start | bytes 6291464 | tf_op jit(solution)/shard_map/ppermute | solution.py:20
  77.4 4.6 %copy-start = (bf16[256,2,4,512]{3,2,1,0:T(4,128)(2,1)}, bf16[256,2,4,512]{3,2,1,0:T(4,128)(2,1)S(1)}, u32[]{:S(2)}) copy-start(bf16[256,2,4,512]{3,2,1,0:T(4,128)(2,1)S(1)} %collective-permute-done) | copy-start | bytes 6291460
  82.1 94.0 %collective-permute-start.1 = (bf16[512,2,4,512]{3,2,1,0:T(4,128)(2,1)}, bf16[512,2,4,512]{3,2,1,0:T(4,128)(2,1)}, u32[]{:S(2)}, u32[]{:S(2)}) collective-permute-start(bf16[512,2,4,512]{3,2,1,0:T(4,128)(2,1)} %pad_maximum_fusion.2), channel_id=1, source_target_pairs={{4,0},{6,2},{8,4},{10,6},{12,8},{14,10},{16,12},{18,14},{20,16},{2... | collective-permute-start | bytes 12582920 | tf_op jit(solution)/shard_map/ppermute | solution.py:20
  83.5 6.1 %collective-permute-start.2 = (bf16[2,512]{1,0:T(2,128)(2,1)S(1)}, bf16[2,512]{1,0:T(2,128)(2,1)S(1)}, u32[]{:S(2)}, u32[]{:S(2)}) collective-permute-start(bf16[2,512]{1,0:T(2,128)(2,1)S(1)} %and_convert_fusion), channel_id=1, source_target_pairs={{2,0},{4,2},{6,4},{8,6},{10,8},{12,10},{14,12},{16,14},{18,16},{20... | collective-permute-start | bytes 6152 | tf_op jit(solution)/shard_map/ppermute | solution.py:20
  89.6 86.5 %collective-permute-start.3 = (bf16[4,512]{1,0:T(4,128)(2,1)S(1)}, bf16[4,512]{1,0:T(4,128)(2,1)S(1)}, u32[]{:S(2)}, u32[]{:S(2)}) collective-permute-start(bf16[4,512]{1,0:T(4,128)(2,1)S(1)} %pad_maximum_fusion.4), channel_id=1, source_target_pairs={{4,0},{6,2},{8,4},{10,6},{12,8},{14,10},{16,12},{18,14},{20,16},{2... | collective-permute-start | bytes 12296 | tf_op jit(solution)/shard_map/ppermute | solution.py:20
Sparse Core Ops, SparseCore 0:
  202.9 66.2 reduce-scatter.1
where the time goes:
time: 277 us; the launch traced here: 276 us
  waiting for transfers between devices  205 us (74%)
  other arithmetic  31.1 us (11%)
  local copies, waits for them, and re-layouts  16.9 us (6%)
  between operations  13.6 us (5%)
  starting transfers between devices  5.46 us (2%)
    ppermute x4, waiting for transfers between devices, shifted(): return lax.ppermute(x, axis, pairs)  138 us
    reduce_scatter x1, waiting for transfers between devices, per_device(): lax.psum_scatter(lax.fori_loop(0, live_rows, add_pair, initial), 'day', s...  66.4 us
    concatenate x2, other arithmetic, per_device(): window = jnp.concatenate([window, arrived], axis=0)  12.8 us
    sqrt x2, local copies, waits for them, and re-layouts, whiten(): jnp.sqrt(values[:, 0] * values[:, 0] + values[:, 1] * values[:, 1])  6.43 us
  transfers between devices with their start and end apart: 5, of which 4 were waited for; matrix products, arithmetic and copies ran while one was open for 0% of the time, Pallas kernels for 0%

commit v1 on v0

v1 whole, which is shorter than its diff:
```python
import functools
import math

import jax
import jax.numpy as jnp
from jax import lax
from jax.experimental import pallas as pl
from jax.experimental.pallas import tpu as pltpu
from jax.sharding import PartitionSpec as P

BLK_DEV = 2
SEGLEN = 15000
FIRST = 90
HALF_WIN = 64
LSTEP = 25
REACH = 3
MESH = pl.DeviceIdType.MESH
VMEM = pl.BlockSpec(memory_space=pltpu.VMEM)
SMEM = pl.BlockSpec(memory_space=pltpu.SMEM)


def phase_tables(lag_total, bin_count):
    lag_index = jnp.arange(lag_total, dtype=jnp.int32)
    lag_samples = (lag_index - lag_total // 2) * LSTEP
    bin_number = FIRST + jnp.arange(bin_count, dtype=jnp.int32)
    phase_turns = lag_samples[:, None] * bin_number[None, :] % SEGLEN
    phase_angle = phase_turns.astype(jnp.float32) * (2.0 * math.pi / SEGLEN)
    return jnp.stack([jnp.cos(phase_angle), jnp.sin(phase_angle)], axis=1)


def mixed(index, offset):
    result = index
    bit = 1
    while bit <= offset:
        if offset & bit:
            result = result + bit - 2 * bit * ((index // bit) % 2)
        bit *= 2
    return result


def whiten_kernel(low_ref, high_ref, raw_ref, out_ref, spread_ref):
    bins = raw_ref.shape[-1]

    @pl.when(pl.program_id(0) == 0)
    def _():
        row = lax.broadcasted_iota(jnp.int32, (bins, bins), 0)
        col = lax.broadcasted_iota(jnp.int32, (bins, bins), 1)
        spread_ref[...] = jnp.where(jnp.abs(row - col) <= HALF_WIN, 1.0, 0.0).astype(jnp.bfloat16)

    bin_index = lax.broadcasted_iota(jnp.int32, (1, bins), 1)
    counts = (
        jnp.minimum(bin_index + HALF_WIN, bins - 1) - jnp.maximum(bin_index - HALF_WIN, 0) + 1
    ).astype(jnp.float32)
    spread = spread_ref[...]
    for block in range(BLK_DEV):
        real = raw_ref[0, 0, block].astype(jnp.float32)
        imag = raw_ref[0, 1, block].astype(jnp.float32)
        magnitude = jnp.sqrt(real * real + imag * imag)
        coarse = magnitude.astype(jnp.bfloat16)
        fine = (magnitude - coarse.astype(jnp.float32)).astype(jnp.bfloat16)
        sums = jnp.dot(coarse, spread, preferred_element_type=jnp.float32) + jnp.dot(
            fine, spread, preferred_element_type=jnp.float32
        )
        amplitude = sums / counts + 1e-05
        keep = (bin_index >= low_ref[block]) & (bin_index < high_ref[block])
        gain = 1.0 / amplitude
        out_ref[0, 0, block] = jnp.where(keep, real * gain, 0.0).astype(jnp.bfloat16)
        out_ref[0, 1, block] = jnp.where(keep, imag * gain, 0.0).astype(jnp.bfloat16)


def gather_kernel(
    tiles, group, pair_ref, own_ref, win_ref, gath_ref,
    send_sem, recv_sem, down_send, down_recv, pair_send, pair_recv, own_sem,
):
    here = lax.axis_index("tile")
    spot = here % group
    base = here - spot
    chunks = 2 * BLK_DEV

    barrier = pltpu.get_barrier_semaphore()
    for offset in range(1, group):
        pl.semaphore_signal(
            barrier, inc=1, device_id={"tile": base + mixed(spot, offset)}, device_id_type=MESH
        )

    @pl.when(base > 0)
    def _():
        pl.semaphore_signal(barrier, inc=1, device_id={"tile": here - group}, device_id_type=MESH)

    @pl.when(base + group < tiles)
    def _():
        pl.semaphore_signal(barrier, inc=1, device_id={"tile": here + group}, device_id_type=MESH)

    peers = group - 1 + (base > 0).astype(jnp.int32) + (base + group < tiles).astype(jnp.int32)
    pl.semaphore_wait(barrier, peers)

    def across(offset, chunk):
        part, block = divmod(chunk, BLK_DEV)
        there = mixed(spot, offset)
        return pltpu.make_async_remote_copy(
            src_ref=own_ref.at[there, part, block],
            dst_ref=win_ref.at[spot, part, block],
            send_sem=send_sem.at[offset - 1, chunk],
            recv_sem=recv_sem.at[offset - 1, chunk],
            device_id={"tile": base + there},
            device_id_type=MESH,
        )

    def pairs_across(offset):
        return pltpu.make_async_remote_copy(
            src_ref=pair_ref,
            dst_ref=gath_ref.at[spot],
            send_sem=pair_send.at[offset - 1],
            recv_sem=pair_recv.at[offset - 1],
            device_id={"tile": base + mixed(spot, offset)},
            device_id_type=MESH,
        )

    def down(source, slot, chunk):
        part, block = divmod(chunk, BLK_DEV)
        return pltpu.make_async_remote_copy(
            src_ref=source.at[slot, part, block],
            dst_ref=win_ref.at[group + slot, part, block],
            send_sem=down_send.at[slot, chunk],
            recv_sem=down_recv.at[slot, chunk],
            device_id={"tile": here - group},
            device_id_type=MESH,
        )

    for offset in range(1, group):
        pairs_across(offset).start()
    for chunk in range(chunks):
        for offset in range(1, group):
            across(offset, chunk).start()

    sends_own = (base > 0) & (spot < REACH)

    @pl.when(sends_own)
    def _():
        for chunk in range(chunks):
            down(own_ref, spot, chunk).start()

    stay = pltpu.make_async_copy(own_ref.at[spot], win_ref.at[spot], own_sem)
    stay.start()
    gath_ref[spot] = pair_ref[...]

    for chunk in range(chunks):
        for offset in range(1, group):
            across(offset, chunk).wait_recv()
            there = mixed(spot, offset)

            @pl.when((base > 0) & (there < REACH))
            def _():
                down(win_ref, there, chunk).start()

    for chunk in range(chunks):
        for offset in range(1, group):
            across(offset, chunk).wait_send()
    for offset in range(1, group):
        pairs_across(offset).wait()
    stay.wait()

    @pl.when(base > 0)
    def _():
        for slot in range(REACH):
            for chunk in range(chunks):
                down(win_ref, slot, chunk).wait_send()

    @pl.when(base + group < tiles)
    def _():
        for slot in range(REACH):
            for chunk in range(chunks):
                down(win_ref, slot, chunk).wait_recv()


def pair_kernel(group, lags, rows_dev, norm_factor, pair_ref, trig_ref, win_ref, out_ref, rot_ref):
    base_block = (lax.axis_index("tile") // group) * group * BLK_DEV
    window_tiles, _, _, chans, _ = win_ref.shape

    def rotate(tile, carry):
        for block in range(BLK_DEV):
            real = win_ref[tile, 0, block].astype(jnp.float32)
            imag = win_ref[tile, 1, block].astype(jnp.float32)
            for lag in range(lags):
                cosine = trig_ref[lag, 0:1]
                sine = trig_ref[lag, 1:2]
                rows = slice(lag * chans, (lag + 1) * chans)
                rot_ref[tile * BLK_DEV + block, 0, rows] = (real * cosine + imag * sine).astype(
                    jnp.bfloat16
                )
                rot_ref[tile * BLK_DEV + block, 1, rows] = (imag * cosine - real * sine).astype(
                    jnp.bfloat16
                )
        return carry

    lax.fori_loop(0, window_tiles, rotate, 0)

    def tile_pairs(tile, carry):
        for row in range(rows_dev):
            first = pair_ref[tile, row, 0]
            second = pair_ref[tile, row, 1]
            left = jnp.maximum(first - base_block, 0)
            right = jnp.maximum(second - base_block, 0)
            total = jnp.zeros((chans, lags * chans), jnp.float32)
            for part in range(2):
                total = total + lax.dot_general(
                    win_ref[left // BLK_DEV, part, left % BLK_DEV],
                    rot_ref[right, part],
                    (((1,), (1,)), ((), ())),
                    preferred_element_type=jnp.float32,
                )
            total = jnp.where(first >= 0, total * norm_factor, 0.0)
            for lag in range(lags):
                out_ref[lag, tile, row] = total[:, lag * chans : (lag + 1) * chans]
        return carry

    lax.fori_loop(0, group, tile_pairs, 0)


def reduce_kernel(
    days, group, part_ref, out_ref, day_buf, send_buf, recv_buf,
    day_send, day_recv, tile_send, tile_recv,
):
    here = lax.axis_index("tile")
    day = lax.axis_index("day")
    spot = here % group
    base = here - spot

    barrier = pltpu.get_barrier_semaphore()
    for offset in range(1, days):
        pl.semaphore_signal(
            barrier, inc=1, device_id={"day": (day + offset) % days}, device_id_type=MESH
        )
    for offset in range(1, group):
        pl.semaphore_signal(
            barrier, inc=1, device_id={"tile": base + mixed(spot, offset)}, device_id_type=MESH
        )
    pl.semaphore_wait(barrier, days - 1 + group - 1)

    order = list(range(group - 1, -1, -1))

    def day_copy(step, offset):
        target = (day + step) % days
        there = mixed(spot, offset)
        return pltpu.make_async_remote_copy(
            src_ref=part_ref.at[target, there],
            dst_ref=day_buf.at[step - 1, offset],
            send_sem=day_send.at[step - 1, offset],
            recv_sem=day_recv.at[step - 1, offset],
            device_id={"day": target},
            device_id_type=MESH,
        )

    def tile_copy(offset):
        return pltpu.make_async_remote_copy(
            src_ref=send_buf.at[offset - 1],
            dst_ref=recv_buf.at[offset - 1],
            send_sem=tile_send.at[offset - 1],
            recv_sem=tile_recv.at[offset - 1],
            device_id={"tile": base + mixed(spot, offset)},
            device_id_type=MESH,
        )

    for offset in order:
        for step in range(1, days):
            day_copy(step, offset).start()
    for offset in order:
        total = part_ref[day, mixed(spot, offset)]
        for step in range(1, days):
            day_copy(step, offset).wait_recv()
            total = total + day_buf[step - 1, offset]
        if offset:
            send_buf[offset - 1] = total.astype(jnp.bfloat16)
            tile_copy(offset).start()
        else:
            out_ref[0] = total
    for offset in order[:-1]:
        tile_copy(offset).wait()
        out_ref[0] += recv_buf[offset - 1].astype(jnp.float32)
    for offset in order:
        for step in range(1, days):
            day_copy(step, offset).wait_send()


def per_device(tiles, days, spectra, band_low, band_high, pair_list):
    own = spectra[0]
    channels, parts, segments, bins = own.shape
    group = segments
    chans = channels // BLK_DEV
    rows_dev = pair_list.shape[0]
    lags = days
    norm_factor = 1.0 / math.sqrt(segments * bins * days)
    slice_shape = (parts, BLK_DEV, chans, bins)
    raw = jnp.transpose(own.reshape(BLK_DEV, chans, parts, segments, bins), (3, 2, 0, 1, 4))

    whitened = pl.pallas_call(
        whiten_kernel,
        grid=(segments,),
        out_shape=jax.ShapeDtypeStruct((segments,) + slice_shape, jnp.bfloat16),
        in_specs=[SMEM, SMEM, pl.BlockSpec((1,) + slice_shape, lambda s: (s, 0, 0, 0, 0))],
        out_specs=pl.BlockSpec((1,) + slice_shape, lambda s: (s, 0, 0, 0, 0)),
        scratch_shapes=[pltpu.VMEM((bins, bins), jnp.bfloat16)],
    )(band_low, band_high, raw)

    padded = jnp.pad(pair_list, ((0, 8 - rows_dev), (0, 126)), constant_values=-1)
    chunks = 2 * BLK_DEV
    window, gathered = pl.pallas_call(
        functools.partial(gather_kernel, tiles, group),
        out_shape=[
            jax.ShapeDtypeStruct((group + REACH,) + slice_shape, jnp.bfloat16),
            jax.ShapeDtypeStruct((group,) + padded.shape, jnp.int32),
        ],
        in_specs=[VMEM, VMEM],
        out_specs=[VMEM, VMEM],
        scratch_shapes=[
            pltpu.SemaphoreType.DMA((group - 1, chunks)),
            pltpu.SemaphoreType.DMA((group - 1, chunks)),
            pltpu.SemaphoreType.DMA((REACH, chunks)),
            pltpu.SemaphoreType.DMA((REACH, chunks)),
            pltpu.SemaphoreType.DMA((group - 1,)),
            pltpu.SemaphoreType.DMA((group - 1,)),
            pltpu.SemaphoreType.DMA,
        ],
        compiler_params=pltpu.CompilerParams(collective_id=0, has_side_effects=True),
    )(padded, whitened)

    partial = pl.pallas_call(
        functools.partial(pair_kernel, group, lags, rows_dev, norm_factor),
        out_shape=jax.ShapeDtypeStruct((lags, group, rows_dev, chans, chans), jnp.float32),
        in_specs=[SMEM, VMEM, VMEM],
        out_specs=VMEM,
        scratch_shapes=[
            pltpu.VMEM(((group + REACH) * BLK_DEV, parts, lags * chans, bins), jnp.bfloat16)
        ],
        compiler_params=pltpu.CompilerParams(vmem_limit_bytes=60 * 1024 * 1024),
    )(gathered, phase_tables(lags, bins), window)

    block_shape = (rows_dev, chans, chans)
    return pl.pallas_call(
        functools.partial(reduce_kernel, days, group),
        out_shape=jax.ShapeDtypeStruct((1,) + block_shape, jnp.float32),
        in_specs=[VMEM],
        out_specs=VMEM,
        scratch_shapes=[
            pltpu.VMEM((days - 1, group) + block_shape, jnp.float32),
            pltpu.VMEM((group - 1,) + block_shape, jnp.bfloat16),
            pltpu.VMEM((group - 1,) + block_shape, jnp.bfloat16),
            pltpu.SemaphoreType.DMA((days - 1, group)),
            pltpu.SemaphoreType.DMA((days - 1, group)),
            pltpu.SemaphoreType.DMA((group - 1,)),
            pltpu.SemaphoreType.DMA((group - 1,)),
        ],
        compiler_params=pltpu.CompilerParams(collective_id=1, has_side_effects=True),
    )(partial)


def solution(mesh):
    placed = (P("day", "tile", None, None, None), P("tile"), P("tile"), P("tile", None))
    return jax.shard_map(
        functools.partial(per_device, mesh.shape["tile"], mesh.shape["day"]),
        mesh=mesh,
        in_specs=placed,
        out_specs=P("day", "tile", None, None),
        check_vma=False,
    )
```

time: 277 us -> 79.8 us (0.29)
  waiting for transfers between devices: 205 us -> 0 us
  Pallas kernels: 0 us -> 71.9 us
  other arithmetic: 31.1 us -> 0.84 us
  between operations: 13.6 us -> 0.03 us
  local copies, waits for them, and re-layouts: 16.9 us -> 6.63 us
  starting transfers between devices: 5.46 us -> 0 us
    ppermute x4 -> x0, waiting for transfers between devices: 138 us -> none  [shifted(): return lax.ppermute(x, axis, pairs)]
    pallas_call x0 -> x4, Pallas kernels: none -> 71.9 us  [the longest x1 43.5 us: per_device(): pl.pallas_call(functools.partial(gather_kernel, tiles, group), out_shape=...]
    reduce_scatter x1 -> x0, waiting for transfers between devices: 66.4 us -> none  [per_device(): lax.psum_scatter(lax.fori_loop(0, live_rows, add_pair, initial), 'day', s...]
    concatenate x4 -> x0, other arithmetic: 12.9 us -> none  [the longest x2 12.8 us: per_device(): window = jnp.concatenate([window, arrived], axis=0)]
    convert_element_type x5 -> x0, other arithmetic: 9.6 us -> none  [the longest x1 3.38 us: whiten(): return (values / amplitude[:, None]).astype(jnp.bfloat16)]
    sqrt x2 -> x0, local copies, waits for them, and re-layouts: 6.43 us -> none  [whiten(): jnp.sqrt(values[:, 0] * values[:, 0] + values[:, 1] * values[:, 1])]
    unnamed x9 -> x3, local copies, waits for them, and re-layouts: 0.03 us -> 6.03 us
    ppermute x4 -> x0, starting transfers between devices: 5.46 us -> none  [shifted(): return lax.ppermute(x, axis, pairs)]
  transfers between devices with their start and end apart: 5 -> 0, of which waited for: 4 -> 0; matrix products, arithmetic and copies ran while one was open for 0% -> 0% of each run, Pallas kernels for 0% -> 0%
where the time goes in v1:
time: 79.8 us; the launch traced here: 79.4 us
  Pallas kernels  71.9 us (90%)
  local copies, waits for them, and re-layouts  6.63 us (8%)
  other arithmetic  0.84 us (1%)
    pallas_call x1, Pallas kernels, per_device(): pl.pallas_call(functools.partial(gather_kernel, tiles, group), out_shape=...  43.5 us
    pallas_call x1, Pallas kernels, per_device(): pl.pallas_call(functools.partial(reduce_kernel, days, group), out_shape=j...  14.9 us
    pallas_call x1, Pallas kernels, per_device(): pl.pallas_call(functools.partial(pair_kernel, group, lags, rows_dev, norm...  8.58 us
    unnamed x3, local copies, waits for them, and re-layouts  6.03 us
    pallas_call x1, Pallas kernels, per_device(): pl.pallas_call(whiten_kernel, grid=(segments,), out_shape=jax.ShapeDtypeS...  4.96 us

profile of v1, /device:TPU:0, one launch (start us, length us, event | category | flops | bytes accessed | tf_op | source)
XLA Modules:
  0.0 79.4 jit_solution(5391756867999378776)
XLA Ops:
  0.0 0.8 copy.5
  0.8 0.6 pad.4.pair_ref
  1.4 3.6 %copy.6 = bf16[1,256,2,4,512]{4,1,2,3,0:T(8,128)(2,1)} copy(bf16[1,256,2,4,512]{4,3,2,1,0:T(4,128)(2,1)} %param.4) | data formatting | bytes 4194304 | tf_op args[0]
  5.0 5.0 %shard_map.46.own_ref = bf16[4,2,2,128,512]{4,3,2,1,0:T(8,128)(2,1)} custom-call(s32[2]{0:T(128)} %low_ref.1, s32[2]{0:T(128)} %high_ref.1, bf16[4,2,2,128,512]{4,3,2,1,0:T(8,128)(2,1)} %bitcast.3), custom_call_target="tpu_custom_call" | custom-call | tf_op jit(solution)/shard_map/pallas_call | solution.py:296
  9.9 43.5 %shard_map.47 = (bf16[7,2,2,128,512]{4,3,2,1,0:T(8,128)(2,1)}, s32[4,8,128]{2,1,0:T(8,128)}) custom-call(s32[8,128]{1,0:T(8,128)} %pad.4.pair_ref, bf16[4,2,2,128,512]{4,3,2,1,0:T(8,128)(2,1)} %shard_map.46.own_ref), custom_call_target="tpu_custom_call" | custom-call | tf_op jit(solution)/shard_map/pallas_call | solution.py:307
  53.4 0.2 fusion.3
  53.7 0.6 pad_maximum_fusion.trig_ref
  54.3 8.6 %shard_map.48.part_ref = f32[2,4,4,128,128]{4,3,2,1,0:T(8,128)} custom-call(s32[4,8,128]{2,1,0:T(8,128)} %get-tuple-element.7.pair_ref, f32[2,2,512]{2,1,0:T(2,128)} %pad_maximum_fusion.trig_ref, bf16[7,2,2,128,512]{4,3,2,1,0:T(8,128)(2,1)} %get-tuple-element.8.win_ref), custom_call_target="tpu_custom_call" | custom-call | tf_op jit(solution)/shard_map/pallas_call | solution.py:327
  62.9 14.9 %shard_map.49 = f32[1,4,128,128]{3,2,1,0:T(8,128)} custom-call(f32[2,4,4,128,128]{4,3,2,1,0:T(8,128)} %shard_map.48.part_ref), custom_call_target="tpu_custom_call" | custom-call | tf_op jit(solution)/shard_map/pallas_call | solution.py:339
  77.7 1.7 %copy.8 = f32[1,4,128,128]{3,2,1,0:T(8,128)} copy(f32[1,4,128,128]{3,2,1,0:T(8,128)} %shard_map.49) | data formatting | bytes 524288
  (2 shorter events, 0.0 us)

commit v2 on v1

v2 whole, which is shorter than its diff:
```python
import functools
import math

import jax
import jax.numpy as jnp
from jax import lax
from jax.experimental import pallas as pl
from jax.experimental.pallas import tpu as pltpu
from jax.sharding import PartitionSpec as P

BLK_DEV = 2
SEGLEN = 15000
FIRST = 90
HALF_WIN = 64
LSTEP = 25
REACH = 3
BELOW = 1
MESH = pl.DeviceIdType.MESH
VMEM = pl.BlockSpec(memory_space=pltpu.VMEM)
SMEM = pl.BlockSpec(memory_space=pltpu.SMEM)


def phase_tables(lag_total, bin_count):
    lag_index = jnp.arange(lag_total, dtype=jnp.int32)
    lag_samples = (lag_index - lag_total // 2) * LSTEP
    bin_number = FIRST + jnp.arange(bin_count, dtype=jnp.int32)
    phase_turns = lag_samples[:, None] * bin_number[None, :] % SEGLEN
    phase_angle = phase_turns.astype(jnp.float32) * (2.0 * math.pi / SEGLEN)
    return jnp.stack([jnp.cos(phase_angle), jnp.sin(phase_angle)], axis=1)


def mixed(index, offset):
    result = index
    bit = 1
    while bit <= offset:
        if offset & bit:
            result = result + bit - 2 * bit * ((index // bit) % 2)
        bit *= 2
    return result


def whiten_kernel(low_ref, high_ref, raw_ref, out_ref, spread_ref):
    bins = raw_ref.shape[-1]

    @pl.when(pl.program_id(0) == 0)
    def _():
        row = lax.broadcasted_iota(jnp.int32, (bins, bins), 0)
        col = lax.broadcasted_iota(jnp.int32, (bins, bins), 1)
        spread_ref[...] = jnp.where(jnp.abs(row - col) <= HALF_WIN, 1.0, 0.0).astype(jnp.bfloat16)

    bin_index = lax.broadcasted_iota(jnp.int32, (1, bins), 1)
    counts = (
        jnp.minimum(bin_index + HALF_WIN, bins - 1) - jnp.maximum(bin_index - HALF_WIN, 0) + 1
    ).astype(jnp.float32)
    spread = spread_ref[...]
    for block in range(BLK_DEV):
        real = raw_ref[0, 0, block].astype(jnp.float32)
        imag = raw_ref[0, 1, block].astype(jnp.float32)
        magnitude = jnp.sqrt(real * real + imag * imag)
        coarse = magnitude.astype(jnp.bfloat16)
        fine = (magnitude - coarse.astype(jnp.float32)).astype(jnp.bfloat16)
        sums = jnp.dot(coarse, spread, preferred_element_type=jnp.float32) + jnp.dot(
            fine, spread, preferred_element_type=jnp.float32
        )
        amplitude = sums / counts + 1e-05
        keep = (bin_index >= low_ref[block]) & (bin_index < high_ref[block])
        gain = 1.0 / amplitude
        out_ref[0, 0, block] = jnp.where(keep, real * gain, 0.0).astype(jnp.bfloat16)
        out_ref[0, 1, block] = jnp.where(keep, imag * gain, 0.0).astype(jnp.bfloat16)


def gather_kernel(
    tiles, group, pair_ref, own_ref, win_ref, gath_ref,
    send_sem, recv_sem, far_send, far_recv, pair_send, pair_recv, up_send, up_recv, own_sem,
):
    here = lax.axis_index("tile")
    spot = here % group
    base = here - spot
    chunks = 2 * BLK_DEV
    has_below = base > 0
    has_above = base + group < tiles
    upper = REACH - BELOW

    barrier = pltpu.get_barrier_semaphore()
    for offset in range(1, group):
        pl.semaphore_signal(
            barrier, inc=1, device_id={"tile": base + mixed(spot, offset)}, device_id_type=MESH
        )

    @pl.when(has_below)
    def _():
        pl.semaphore_signal(barrier, inc=1, device_id={"tile": here - group}, device_id_type=MESH)

    @pl.when(has_above)
    def _():
        pl.semaphore_signal(barrier, inc=1, device_id={"tile": here + group}, device_id_type=MESH)

    peers = group - 1 + has_below.astype(jnp.int32) + has_above.astype(jnp.int32)
    pl.semaphore_wait(barrier, peers)

    def across(offset, chunk):
        part, block = divmod(chunk, BLK_DEV)
        there = mixed(spot, offset)
        return pltpu.make_async_remote_copy(
            src_ref=own_ref.at[there, part, block],
            dst_ref=win_ref.at[BELOW + spot, part, block],
            send_sem=send_sem.at[offset - 1, chunk],
            recv_sem=recv_sem.at[offset - 1, chunk],
            device_id={"tile": base + there},
            device_id_type=MESH,
        )

    def pairs_across(offset):
        return pltpu.make_async_remote_copy(
            src_ref=pair_ref,
            dst_ref=gath_ref.at[BELOW + spot],
            send_sem=pair_send.at[offset - 1],
            recv_sem=pair_recv.at[offset - 1],
            device_id={"tile": base + mixed(spot, offset)},
            device_id_type=MESH,
        )

    def pairs_up():
        return pltpu.make_async_remote_copy(
            src_ref=gath_ref.at[group],
            dst_ref=gath_ref.at[0],
            send_sem=up_send,
            recv_sem=up_recv,
            device_id={"tile": here + group},
            device_id_type=MESH,
        )

    def far(source, slot, target, device, chunk):
        part, block = divmod(chunk, BLK_DEV)
        index = 0 if target == 0 else target - BELOW - group + 1
        return pltpu.make_async_remote_copy(
            src_ref=source.at[slot, part, block],
            dst_ref=win_ref.at[target, part, block],
            send_sem=far_send.at[index, chunk],
            recv_sem=far_recv.at[index, chunk],
            device_id={"tile": device},
            device_id_type=MESH,
        )

    def relay(source, slot, where, chunk_list):
        for lower in range(upper):

            @pl.when(has_below & (where == lower))
            def _():
                for chunk in chunk_list:
                    far(source, slot, BELOW + group + lower, here - group, chunk).start()

        @pl.when(has_above & (where == group - 1))
        def _():
            for chunk in chunk_list:
                far(source, slot, 0, here + group, chunk).start()

    for offset in range(1, group):
        pairs_across(offset).start()
    for chunk in range(chunks):
        for offset in range(1, group):
            across(offset, chunk).start()
    relay(own_ref, spot, spot, range(chunks))
    stay = pltpu.make_async_copy(own_ref.at[spot], win_ref.at[BELOW + spot], own_sem)
    stay.start()
    gath_ref[BELOW + spot] = pair_ref[...]

    for chunk in range(chunks):
        for offset in range(1, group):
            across(offset, chunk).wait_recv()
            there = mixed(spot, offset)
            relay(win_ref, BELOW + there, there, [chunk])

    for chunk in range(chunks):
        for offset in range(1, group):
            across(offset, chunk).wait_send()
    stay.wait()
    for offset in range(1, group):
        pairs_across(offset).wait()

    @pl.when(has_above)
    def _():
        pairs_up().start()
        pairs_up().wait_send()
        for chunk in range(chunks):
            far(own_ref, 0, 0, here + group, chunk).wait_send()
            for lower in range(upper):
                far(own_ref, 0, BELOW + group + lower, here, chunk).wait_recv()

    @pl.when(has_below)
    def _():
        pairs_up().wait_recv()
        for chunk in range(chunks):
            far(own_ref, 0, 0, here, chunk).wait_recv()
            for lower in range(upper):
                far(own_ref, 0, BELOW + group + lower, here - group, chunk).wait_send()

    @pl.when(base == 0)
    def _():
        gath_ref[0] = jnp.full(pair_ref.shape, -1, jnp.int32)


def pair_kernel(
    tiles, days, group, norm_factor, pair_ref, trig_ref, win_ref, out_ref,
    rot_ref, part_ref, day_buf, send_buf, recv_buf, top_buf, down_src, down_buf,
    day_send, day_recv, tile_send, tile_recv, top_send, top_recv, down_send, down_recv,
):
    here = lax.axis_index("tile")
    day = lax.axis_index("day")
    spot = here % group
    base = here - spot
    last = group - 1
    has_below = base > 0
    has_above = base + group < tiles
    is_top = base + group == tiles
    base_block = (base - BELOW) * BLK_DEV
    window_tiles, _, _, chans, _ = win_ref.shape
    lags = days
    rows_dev = out_ref.shape[1]

    barrier = pltpu.get_barrier_semaphore()
    for offset in range(1, days):
        pl.semaphore_signal(
            barrier, inc=1, device_id={"day": (day + offset) % days}, device_id_type=MESH
        )
    for offset in range(1, group):
        pl.semaphore_signal(
            barrier, inc=1, device_id={"tile": base + mixed(spot, offset)}, device_id_type=MESH
        )

    @pl.when(has_below)
    def _():
        pl.semaphore_signal(barrier, inc=1, device_id={"tile": here - group}, device_id_type=MESH)

    @pl.when(has_above)
    def _():
        pl.semaphore_signal(barrier, inc=1, device_id={"tile": here + group}, device_id_type=MESH)

    def rotate(tile, carry):
        for block in range(BLK_DEV):
            real = win_ref[tile, 0, block].astype(jnp.float32)
            imag = win_ref[tile, 1, block].astype(jnp.float32)
            for lag in range(lags):
                cosine = trig_ref[lag, 0:1]
                sine = trig_ref[lag, 1:2]
                rows = slice(lag * chans, (lag + 1) * chans)
                rot_ref[tile * BLK_DEV + block, 0, rows] = (real * cosine + imag * sine).astype(
                    jnp.bfloat16
                )
                rot_ref[tile * BLK_DEV + block, 1, rows] = (imag * cosine - real * sine).astype(
                    jnp.bfloat16
                )
        return carry

    lax.fori_loop(0, window_tiles, rotate, 0)
    peers = days - 1 + last + has_below.astype(jnp.int32) + has_above.astype(jnp.int32)
    pl.semaphore_wait(barrier, peers)

    def products(set_index, slot):
        for row in range(rows_dev):
            first = pair_ref[set_index, row, 0]
            second = pair_ref[set_index, row, 1]
            left = jnp.clip(first - base_block, 0, window_tiles * BLK_DEV - 1)
            right = jnp.clip(second - base_block, 0, window_tiles * BLK_DEV - 1)
            total = jnp.zeros((chans, lags * chans), jnp.float32)
            for part in range(2):
                total = total + lax.dot_general(
                    win_ref[left // BLK_DEV, part, left % BLK_DEV],
                    rot_ref[right, part],
                    (((1,), (1,)), ((), ())),
                    preferred_element_type=jnp.float32,
                )
            total = jnp.where(first >= 0, total * norm_factor, 0.0)
            for lag in range(lags):
                part_ref[slot, lag, row] = total[:, lag * chans : (lag + 1) * chans]

    def day_copy(step, slot):
        target = (day + step) % days
        return pltpu.make_async_remote_copy(
            src_ref=part_ref.at[slot, target],
            dst_ref=day_buf.at[step - 1, slot],
            send_sem=day_send.at[step - 1, slot],
            recv_sem=day_recv.at[step - 1, slot],
            device_id={"day": target},
            device_id_type=MESH,
        )

    def day_total(slot):
        total = part_ref[slot, day]
        for step in range(1, days):
            day_copy(step, slot).wait_recv()
            total = total + day_buf[step - 1, slot]
        return total

    def tile_copy(offset):
        return pltpu.make_async_remote_copy(
            src_ref=send_buf.at[offset - 1],
            dst_ref=recv_buf.at[offset - 1],
            send_sem=tile_send.at[offset - 1],
            recv_sem=tile_recv.at[offset - 1],
            device_id={"tile": base + mixed(spot, offset)},
            device_id_type=MESH,
        )

    def top_copy(device, slot):
        return pltpu.make_async_remote_copy(
            src_ref=send_buf.at[last],
            dst_ref=top_buf.at[slot],
            send_sem=top_send,
            recv_sem=top_recv.at[slot],
            device_id={"tile": device},
            device_id_type=MESH,
        )

    def down_copy(row, device):
        return pltpu.make_async_remote_copy(
            src_ref=down_src.at[row],
            dst_ref=down_buf.at[row],
            send_sem=down_send.at[row],
            recv_sem=down_recv.at[row],
            device_id={"tile": device},
            device_id_type=MESH,
        )

    def push(offset):
        send_buf[offset - 1] = day_total(offset).astype(jnp.bfloat16)
        tile_copy(offset).start()

    for offset in range(last, -1, -1):
        products((mixed(spot, offset) + BELOW) % group, offset)
        for step in range(1, days):
            day_copy(step, offset).start()
        if offset < last:
            push(offset + 1)

    @pl.when(is_top)
    def _():
        products(group, group)
        for step in range(1, days):
            day_copy(step, group).start()

    out_ref[0] = day_total(0)

    @pl.when(is_top)
    def _():
        total = day_total(group)

        @pl.when(spot < last)
        def _():
            send_buf[last] = total.astype(jnp.bfloat16)
            top_copy(base + last, spot).start()

        @pl.when(spot == last)
        def _():
            down_buf[...] = total

    for offset in range(last, 0, -1):
        tile_copy(offset).wait_recv()
    sends_down = has_below & (spot == last)
    takes_down = has_above & (spot == last)
    for row in range(rows_dev):
        total = out_ref[0, row]
        for offset in range(last, 0, -1):
            total = total + recv_buf[offset - 1, row].astype(jnp.float32)
        out_ref[0, row] = total

        @pl.when(sends_down)
        def _():
            down_src[row] = total
            down_copy(row, here - group).start()

    @pl.when(takes_down)
    def _():
        for row in range(rows_dev):
            down_copy(row, here).wait_recv()
            out_ref[0, row] = down_buf[row]

    @pl.when(is_top & (spot == last))
    def _():
        total = down_buf[...]
        for slot in range(last):
            top_copy(here, slot).wait_recv()
            total = total + top_buf[slot].astype(jnp.float32)
        out_ref[0] = total

    @pl.when(is_top & (spot < last))
    def _():
        top_copy(base + last, spot).wait_send()

    @pl.when(sends_down)
    def _():
        for row in range(rows_dev):
            down_copy(row, here - group).wait_send()

    for offset in range(last, 0, -1):
        tile_copy(offset).wait_send()
    for offset in range(last, -1, -1):
        for step in range(1, days):
            day_copy(step, offset).wait_send()

    @pl.when(is_top)
    def _():
        for step in range(1, days):
            day_copy(step, group).wait_send()


def per_device(tiles, days, spectra, band_low, band_high, pair_list):
    own = spectra[0]
    channels, parts, segments, bins = own.shape
    group = segments
    chans = channels // BLK_DEV
    rows_dev = pair_list.shape[0]
    lags = days
    norm_factor = 1.0 / math.sqrt(segments * bins * days)
    slice_shape = (parts, BLK_DEV, chans, bins)
    raw = jnp.transpose(own.reshape(BLK_DEV, chans, parts, segments, bins), (3, 2, 0, 1, 4))

    whitened = pl.pallas_call(
        whiten_kernel,
        grid=(segments,),
        out_shape=jax.ShapeDtypeStruct((segments,) + slice_shape, jnp.bfloat16),
        in_specs=[SMEM, SMEM, pl.BlockSpec((1,) + slice_shape, lambda s: (s, 0, 0, 0, 0))],
        out_specs=pl.BlockSpec((1,) + slice_shape, lambda s: (s, 0, 0, 0, 0)),
        scratch_shapes=[pltpu.VMEM((bins, bins), jnp.bfloat16)],
    )(band_low, band_high, raw)

    padded = jnp.pad(pair_list, ((0, 8 - rows_dev), (0, 126)), constant_values=-1)
    chunks = 2 * BLK_DEV
    window, gathered = pl.pallas_call(
        functools.partial(gather_kernel, tiles, group),
        out_shape=[
            jax.ShapeDtypeStruct((group + REACH,) + slice_shape, jnp.bfloat16),
            jax.ShapeDtypeStruct((BELOW + group,) + padded.shape, jnp.int32),
        ],
        in_specs=[VMEM, VMEM],
        out_specs=[VMEM, VMEM],
        scratch_shapes=[
            pltpu.SemaphoreType.DMA((group - 1, chunks)),
            pltpu.SemaphoreType.DMA((group - 1, chunks)),
            pltpu.SemaphoreType.DMA((REACH, chunks)),
            pltpu.SemaphoreType.DMA((REACH, chunks)),
            pltpu.SemaphoreType.DMA((group - 1,)),
            pltpu.SemaphoreType.DMA((group - 1,)),
            pltpu.SemaphoreType.DMA,
            pltpu.SemaphoreType.DMA,
            pltpu.SemaphoreType.DMA,
        ],
        compiler_params=pltpu.CompilerParams(collective_id=0, has_side_effects=True),
    )(padded, whitened)

    block_shape = (rows_dev, chans, chans)
    return pl.pallas_call(
        functools.partial(pair_kernel, tiles, days, group, norm_factor),
        out_shape=jax.ShapeDtypeStruct((1,) + block_shape, jnp.float32),
        in_specs=[SMEM, VMEM, VMEM],
        out_specs=VMEM,
        scratch_shapes=[
            pltpu.VMEM(((group + REACH) * BLK_DEV, parts, lags * chans, bins), jnp.bfloat16),
            pltpu.VMEM((group + 1, lags) + block_shape, jnp.float32),
            pltpu.VMEM((days - 1, group + 1) + block_shape, jnp.float32),
            pltpu.VMEM((group,) + block_shape, jnp.bfloat16),
            pltpu.VMEM((group - 1,) + block_shape, jnp.bfloat16),
            pltpu.VMEM((group - 1,) + block_shape, jnp.bfloat16),
            pltpu.VMEM(block_shape, jnp.float32),
            pltpu.VMEM(block_shape, jnp.float32),
            pltpu.SemaphoreType.DMA((days - 1, group + 1)),
            pltpu.SemaphoreType.DMA((days - 1, group + 1)),
            pltpu.SemaphoreType.DMA((group - 1,)),
            pltpu.SemaphoreType.DMA((group - 1,)),
            pltpu.SemaphoreType.DMA,
            pltpu.SemaphoreType.DMA((group - 1,)),
            pltpu.SemaphoreType.DMA((rows_dev,)),
            pltpu.SemaphoreType.DMA((rows_dev,)),
        ],
        compiler_params=pltpu.CompilerParams(
            collective_id=1, has_side_effects=True, vmem_limit_bytes=63 * 1024 * 1024
        ),
    )(gathered, phase_tables(lags, bins), window)


def solution(mesh):
    placed = (P("day", "tile", None, None, None), P("tile"), P("tile"), P("tile", None))
    return jax.shard_map(
        functools.partial(per_device, mesh.shape["tile"], mesh.shape["day"]),
        mesh=mesh,
        in_specs=placed,
        out_specs=P("day", "tile", None, None),
        check_vma=False,
    )
```

time: 79.8 us -> 72.2 us (0.905)
  the two profiles are of different devices: /device:TPU:0 before, /device:TPU:14 now
where the time goes in v2:
time: 72.2 us; the launch traced here: 71.9 us
  Pallas kernels  64.4 us (89%)
  local copies, waits for them, and re-layouts  6.63 us (9%)
  other arithmetic  0.84 us (1%)
    pallas_call x1, Pallas kernels, per_device(): pl.pallas_call(functools.partial(gather_kernel, tiles, group), out_shape=...  35.5 us
    pallas_call x1, Pallas kernels, per_device(): pl.pallas_call(functools.partial(pair_kernel, tiles, days, group, norm_fa...  24 us
    unnamed x3, local copies, waits for them, and re-layouts  6.03 us
    pallas_call x1, Pallas kernels, per_device(): pl.pallas_call(whiten_kernel, grid=(segments,), out_shape=jax.ShapeDtypeS...  4.95 us

profile of v2, /device:TPU:14, one launch (start us, length us, event | category | flops | bytes accessed | tf_op | source)
XLA Modules:
  0.0 71.9 jit_solution(3369812524500050048)
XLA Ops:
  0.0 0.8 %copy.5 = s32[4,2]{1,0:T(4,128)S(1)} copy(s32[4,2]{0,1:T(2,128)} %param.7) | data formatting | bytes 64 | tf_op args[3]
  0.8 0.6 pad.4.pair_ref
  1.4 3.6 %copy.6 = bf16[1,256,2,4,512]{4,1,2,3,0:T(8,128)(2,1)} copy(bf16[1,256,2,4,512]{4,3,2,1,0:T(4,128)(2,1)} %param.4) | data formatting | bytes 4194304 | tf_op args[0]
  5.0 5.0 %shard_map.46.own_ref = bf16[4,2,2,128,512]{4,3,2,1,0:T(8,128)(2,1)} custom-call(s32[2]{0:T(128)} %low_ref.1, s32[2]{0:T(128)} %high_ref.1, bf16[4,2,2,128,512]{4,3,2,1,0:T(8,128)(2,1)} %bitcast.3), custom_call_target="tpu_custom_call" | custom-call | tf_op jit(solution)/shard_map/pallas_call | solution.py:418
  9.9 35.5 %shard_map.47 = (bf16[7,2,2,128,512]{4,3,2,1,0:T(8,128)(2,1)}, s32[5,8,128]{2,1,0:T(8,128)}) custom-call(s32[8,128]{1,0:T(8,128)} %pad.4.pair_ref, bf16[4,2,2,128,512]{4,3,2,1,0:T(8,128)(2,1)} %shard_map.46.own_ref), custom_call_target="tpu_custom_call" | custom-call | tf_op jit(solution)/shard_map/pallas_call | solution.py:429
  45.5 0.2 fusion.3
  45.7 0.6 pad_maximum_fusion.trig_ref
  46.3 24.0 %shard_map.48 = f32[1,4,128,128]{3,2,1,0:T(8,128)} custom-call(s32[5,8,128]{2,1,0:T(8,128)} %get-tuple-element.7.pair_ref, f32[2,2,512]{2,1,0:T(2,128)} %pad_maximum_fusion.trig_ref, bf16[7,2,2,128,512]{4,3,2,1,0:T(8,128)(2,1)} %get-tuple-element.8.win_ref), custom_call_target="tpu_custom_call" | custom-call | tf_op jit(solution)/shard_map/pallas_call | solution.py:452
  70.3 1.7 %copy.8 = f32[1,4,128,128]{3,2,1,0:T(8,128)} copy(f32[1,4,128,128]{3,2,1,0:T(8,128)} %shard_map.48) | data formatting | bytes 524288
  (2 shorter events, 0.0 us)

commit v3 on v2

--- a/solution.py
+++ b/solution.py
@@ -3,6 +3,7 @@
 
 import jax
 import jax.numpy as jnp
+import numpy as np
 from jax import lax
 from jax.experimental import pallas as pl
 from jax.experimental.pallas import tpu as pltpu
@@ -21,12 +22,11 @@
 
 
 def phase_tables(lag_total, bin_count):
-    lag_index = jnp.arange(lag_total, dtype=jnp.int32)
-    lag_samples = (lag_index - lag_total // 2) * LSTEP
-    bin_number = FIRST + jnp.arange(bin_count, dtype=jnp.int32)
+    lag_samples = (np.arange(lag_total) - lag_total // 2) * LSTEP
+    bin_number = FIRST + np.arange(bin_count)
     phase_turns = lag_samples[:, None] * bin_number[None, :] % SEGLEN
-    phase_angle = phase_turns.astype(jnp.float32) * (2.0 * math.pi / SEGLEN)
-    return jnp.stack([jnp.cos(phase_angle), jnp.sin(phase_angle)], axis=1)
+    phase_angle = phase_turns.astype(np.float32) * np.float32(2.0 * math.pi / SEGLEN)
+    return np.stack([np.cos(phase_angle), np.sin(phase_angle)], axis=1).astype(np.float32)
 
 
 def mixed(index, offset):
@@ -39,7 +39,7 @@
     return result
 
 
-def whiten_kernel(low_ref, high_ref, raw_ref, out_ref, spread_ref):
+def whiten_kernel(low_ref, high_ref, pair_ref, raw_ref, out_ref, padded_ref, spread_ref):
     bins = raw_ref.shape[-1]
 
     @pl.when(pl.program_id(0) == 0)
@@ -47,6 +47,13 @@
         row = lax.broadcasted_iota(jnp.int32, (bins, bins), 0)
         col = lax.broadcasted_iota(jnp.int32, (bins, bins), 1)
         spread_ref[...] = jnp.where(jnp.abs(row - col) <= HALF_WIN, 1.0, 0.0).astype(jnp.bfloat16)
+        row = lax.broadcasted_iota(jnp.int32, padded_ref.shape, 0)
+        col = lax.broadcasted_iota(jnp.int32, padded_ref.shape, 1)
+        padded = jnp.full(padded_ref.shape, -1, jnp.int32)
+        for pair in range(pair_ref.shape[0]):
+            for side in range(2):
+                padded = jnp.where((row == pair) & (col == side), pair_ref[pair, side], padded)
+        padded_ref[...] = padded
 
     bin_index = lax.broadcasted_iota(jnp.int32, (1, bins), 1)
     counts = (
@@ -69,11 +76,15 @@
         out_ref[0, 1, block] = jnp.where(keep, imag * gain, 0.0).astype(jnp.bfloat16)
 
 
-def gather_kernel(
-    tiles, group, pair_ref, own_ref, win_ref, gath_ref,
+def correlate_kernel(
+    tiles, days, group, norm_factor, own_pair_ref, trig_ref, own_ref, out_ref,
+    win_ref, gath_ref, pair_ref,
+    rot_ref, part_ref, day_buf, send_buf, recv_buf, top_buf, down_src, down_buf,
     send_sem, recv_sem, far_send, far_recv, pair_send, pair_recv, up_send, up_recv, own_sem,
+    day_send, day_recv, tile_send, tile_recv, top_send, top_recv, down_send, down_recv,
 ):
     here = lax.axis_index("tile")
+    day = lax.axis_index("day")
     spot = here % group
     base = here - spot
     chunks = 2 * BLK_DEV
@@ -81,7 +92,18 @@
     has_above = base + group < tiles
     upper = REACH - BELOW
 
+    last = group - 1
+    is_top = base + group == tiles
+    base_block = (base - BELOW) * BLK_DEV
+    window_tiles, _, _, chans, _ = win_ref.shape
+    lags = days
+    rows_dev = out_ref.shape[1]
+
     barrier = pltpu.get_barrier_semaphore()
+    for offset in range(1, days):
+        pl.semaphore_signal(
+            barrier, inc=1, device_id={"day": (day + offset) % days}, device_id_type=MESH
+        )
     for offset in range(1, group):
         pl.semaphore_signal(
             barrier, inc=1, device_id={"tile": base + mixed(spot, offset)}, device_id_type=MESH
@@ -95,11 +117,11 @@
     def _():
         pl.semaphore_signal(barrier, inc=1, device_id={"tile": here + group}, device_id_type=MESH)
 
-    peers = group - 1 + has_below.astype(jnp.int32) + has_above.astype(jnp.int32)
+    peers = days - 1 + group - 1 + has_below.astype(jnp.int32) + has_above.astype(jnp.int32)
     pl.semaphore_wait(barrier, peers)
 
     def across(offset, chunk):
-        part, block = divmod(chunk, BLK_DEV)
+        block, part = divmod(chunk, 2)
         there = mixed(spot, offset)
         return pltpu.make_async_remote_copy(
             src_ref=own_ref.at[there, part, block],
@@ -112,7 +134,7 @@
 
     def pairs_across(offset):
         return pltpu.make_async_remote_copy(
-            src_ref=pair_ref,
+            src_ref=own_pair_ref,
             dst_ref=gath_ref.at[BELOW + spot],
             send_sem=pair_send.at[offset - 1],
             recv_sem=pair_recv.at[offset - 1],
@@ -131,7 +153,7 @@
         )
 
     def far(source, slot, target, device, chunk):
-        part, block = divmod(chunk, BLK_DEV)
+        block, part = divmod(chunk, 2)
         index = 0 if target == 0 else target - BELOW - group + 1
         return pltpu.make_async_remote_copy(
             src_ref=source.at[slot, part, block],
@@ -163,78 +185,17 @@
     relay(own_ref, spot, spot, range(chunks))
     stay = pltpu.make_async_copy(own_ref.at[spot], win_ref.at[BELOW + spot], own_sem)
     stay.start()
-    gath_ref[BELOW + spot] = pair_ref[...]
+    gath_ref[BELOW + spot] = own_pair_ref[...]
+
+    @pl.when(base == 0)
+    def _():
+        gath_ref[0] = jnp.full(own_pair_ref.shape, -1, jnp.int32)
 
     for chunk in range(chunks):
         for offset in range(1, group):
             across(offset, chunk).wait_recv()
             there = mixed(spot, offset)
             relay(win_ref, BELOW + there, there, [chunk])
-
-    for chunk in range(chunks):
-        for offset in range(1, group):
-            across(offset, chunk).wait_send()
-    stay.wait()
-    for offset in range(1, group):
-        pairs_across(offset).wait()
-
-    @pl.when(has_above)
-    def _():
-        pairs_up().start()
-        pairs_up().wait_send()
-        for chunk in range(chunks):
-            far(own_ref, 0, 0, here + group, chunk).wait_send()
-            for lower in range(upper):
-                far(own_ref, 0, BELOW + group + lower, here, chunk).wait_recv()
-
-    @pl.when(has_below)
-    def _():
-        pairs_up().wait_recv()
-        for chunk in range(chunks):
-            far(own_ref, 0, 0, here, chunk).wait_recv()
-            for lower in range(upper):
-                far(own_ref, 0, BELOW + group + lower, here - group, chunk).wait_send()
-
-    @pl.when(base == 0)
-    def _():
-        gath_ref[0] = jnp.full(pair_ref.shape, -1, jnp.int32)
-
-
-def pair_kernel(
-    tiles, days, group, norm_factor, pair_ref, trig_ref, win_ref, out_ref,
-    rot_ref, part_ref, day_buf, send_buf, recv_buf, top_buf, down_src, down_buf,
-    day_send, day_recv, tile_send, tile_recv, top_send, top_recv, down_send, down_recv,
-):
-    here = lax.axis_index("tile")
-    day = lax.axis_index("day")
-    spot = here % group
-    base = here - spot
-    last = group - 1
-    has_below = base > 0
-    has_above = base + group < tiles
-    is_top = base + group == tiles
-    base_block = (base - BELOW) * BLK_DEV
-    window_tiles, _, _, chans, _ = win_ref.shape
-    lags = days
-    rows_dev = out_ref.shape[1]
-
-    barrier = pltpu.get_barrier_semaphore()
-    for offset in range(1, days):
-        pl.semaphore_signal(
-            barrier, inc=1, device_id={"day": (day + offset) % days}, device_id_type=MESH
-        )
-    for offset in range(1, group):
-        pl.semaphore_signal(
-            barrier, inc=1, device_id={"tile": base + mixed(spot, offset)}, device_id_type=MESH
-        )
-
-    @pl.when(has_below)
-    def _():
-        pl.semaphore_signal(barrier, inc=1, device_id={"tile": here - group}, device_id_type=MESH)
-
-    @pl.when(has_above)
-    def _():
-        pl.semaphore_signal(barrier, inc=1, device_id={"tile": here + group}, device_id_type=MESH)
 
     def rotate(tile, carry):
         for block in range(BLK_DEV):
@@ -252,9 +213,40 @@
                 )
         return carry
 
-    lax.fori_loop(0, window_tiles, rotate, 0)
-    peers = days - 1 + last + has_below.astype(jnp.int32) + has_above.astype(jnp.int32)
-    pl.semaphore_wait(barrier, peers)
+    for chunk in range(chunks):
+        for offset in range(1, group):
+            across(offset, chunk).wait_send()
+    stay.wait()
+    for offset in range(1, group):
+        pairs_across(offset).wait()
+
+    @pl.when(has_above)
+    def _():
+        pairs_up().start()
+
+    lax.fori_loop(BELOW, BELOW + group, rotate, 0)
+
+    @pl.when(has_above)
+    def _():
+        pairs_up().wait_send()
+        for chunk in range(chunks):
+            far(own_ref, 0, 0, here + group, chunk).wait_send()
+            for lower in range(upper):
+                far(own_ref, 0, BELOW + group + lower, here, chunk).wait_recv()
+
+    @pl.when(has_below)
+    def _():
+        pairs_up().wait_recv()
+        for chunk in range(chunks):
+            far(own_ref, 0, 0, here, chunk).wait_recv()
+            for lower in range(upper):
+                far(own_ref, 0, BELOW + group + lower, here - group, chunk).wait_send()
+
+    gather_pairs = pltpu.make_async_copy(gath_ref, pair_ref, own_sem)
+    gather_pairs.start()
+    lax.fori_loop(0, BELOW, rotate, 0)
+    lax.fori_loop(BELOW + group, window_tiles, rotate, 0)
+    gather_pairs.wait()
 
     def products(set_index, slot):
         for row in range(rows_dev):
@@ -415,26 +407,41 @@
     slice_shape = (parts, BLK_DEV, chans, bins)
     raw = jnp.transpose(own.reshape(BLK_DEV, chans, parts, segments, bins), (3, 2, 0, 1, 4))
 
-    whitened = pl.pallas_call(
+    whitened, padded = pl.pallas_call(
         whiten_kernel,
         grid=(segments,),
-        out_shape=jax.ShapeDtypeStruct((segments,) + slice_shape, jnp.bfloat16),
-        in_specs=[SMEM, SMEM, pl.BlockSpec((1,) + slice_shape, lambda s: (s, 0, 0, 0, 0))],
-        out_specs=pl.BlockSpec((1,) + slice_shape, lambda s: (s, 0, 0, 0, 0)),
+        out_shape=[
+            jax.ShapeDtypeStruct((segments,) + slice_shape, jnp.bfloat16),
+            jax.ShapeDtypeStruct((8, 128), jnp.int32),
+        ],
+        in_specs=[SMEM, SMEM, SMEM, pl.BlockSpec((1,) + slice_shape, lambda s: (s, 0, 0, 0, 0))],
+        out_specs=[
+            pl.BlockSpec((1,) + slice_shape, lambda s: (s, 0, 0, 0, 0)),
+            pl.BlockSpec((8, 128), lambda s: (0, 0)),
+        ],
         scratch_shapes=[pltpu.VMEM((bins, bins), jnp.bfloat16)],
-    )(band_low, band_high, raw)
-
-    padded = jnp.pad(pair_list, ((0, 8 - rows_dev), (0, 126)), constant_values=-1)
+    )(band_low, band_high, pair_list, raw)
+
     chunks = 2 * BLK_DEV
-    window, gathered = pl.pallas_call(
-        functools.partial(gather_kernel, tiles, group),
-        out_shape=[
-            jax.ShapeDtypeStruct((group + REACH,) + slice_shape, jnp.bfloat16),
-            jax.ShapeDtypeStruct((BELOW + group,) + padded.shape, jnp.int32),
-        ],
-        in_specs=[VMEM, VMEM],
-        out_specs=[VMEM, VMEM],
+    block_shape = (rows_dev, chans, chans)
+    gathered_shape = (BELOW + group, 8, 128)
+    return pl.pallas_call(
+        functools.partial(correlate_kernel, tiles, days, group, norm_factor),
+        out_shape=jax.ShapeDtypeStruct((1,) + block_shape, jnp.float32),
+        in_specs=[VMEM, VMEM, VMEM],
+        out_specs=VMEM,
         scratch_shapes=[
+            pltpu.VMEM((group + REACH,) + slice_shape, jnp.bfloat16),
+            pltpu.VMEM(gathered_shape, jnp.int32),
+            pltpu.SMEM(gathered_shape, jnp.int32),
+            pltpu.VMEM(((group + REACH) * BLK_DEV, parts, lags * chans, bins), jnp.bfloat16),
+            pltpu.VMEM((group + 1, lags) + block_shape, jnp.float32),
+            pltpu.VMEM((days - 1, group + 1) + block_shape, jnp.float32),
+            pltpu.VMEM((group,) + block_shape, jnp.bfloat16),
+            pltpu.VMEM((group - 1,) + block_shape, jnp.bfloat16),
+            pltpu.VMEM((group - 1,) + block_shape, jnp.bfloat16),
+            pltpu.VMEM(block_shape, jnp.float32),
+            pltpu.VMEM(block_shape, jnp.float32),
             pltpu.SemaphoreType.DMA((group - 1, chunks)),
             pltpu.SemaphoreType.DMA((group - 1, chunks)),
             pltpu.SemaphoreType.DMA((REACH, chunks)),
@@ -444,25 +451,6 @@
             pltpu.SemaphoreType.DMA,
             pltpu.SemaphoreType.DMA,
             pltpu.SemaphoreType.DMA,
-        ],
-        compiler_params=pltpu.CompilerParams(collective_id=0, has_side_effects=True),
-    )(padded, whitened)
-
-    block_shape = (rows_dev, chans, chans)
-    return pl.pallas_call(
-        functools.partial(pair_kernel, tiles, days, group, norm_factor),
-        out_shape=jax.ShapeDtypeStruct((1,) + block_shape, jnp.float32),
-        in_specs=[SMEM, VMEM, VMEM],
-        out_specs=VMEM,
-        scratch_shapes=[
-            pltpu.VMEM(((group + REACH) * BLK_DEV, parts, lags * chans, bins), jnp.bfloat16),
-            pltpu.VMEM((group + 1, lags) + block_shape, jnp.float32),
-            pltpu.VMEM((days - 1, group + 1) + block_shape, jnp.float32),
-            pltpu.VMEM((group,) + block_shape, jnp.bfloat16),
-            pltpu.VMEM((group - 1,) + block_shape, jnp.bfloat16),
-            pltpu.VMEM((group - 1,) + block_shape, jnp.bfloat16),
-            pltpu.VMEM(block_shape, jnp.float32),
-            pltpu.VMEM(block_shape, jnp.float32),
             pltpu.SemaphoreType.DMA((days - 1, group + 1)),
             pltpu.SemaphoreType.DMA((days - 1, group + 1)),
             pltpu.SemaphoreType.DMA((group - 1,)),
@@ -473,9 +461,9 @@
             pltpu.SemaphoreType.DMA((rows_dev,)),
         ],
         compiler_params=pltpu.CompilerParams(
-            collective_id=1, has_side_effects=True, vmem_limit_bytes=63 * 1024 * 1024
+            collective_id=0, has_side_effects=True, vmem_limit_bytes=63 * 1024 * 1024
         ),
-    )(gathered, phase_tables(lags, bins), window)
+    )(padded, jnp.asarray(phase_tables(lags, bins)), whitened)
 
 
 def solution(mesh):

time: 72.2 us -> 66.4 us (0.920)
  Pallas kernels: 64.4 us -> 59.5 us
  other arithmetic: 0.84 us -> 0 us
    pallas_call x3 -> x2, Pallas kernels: 64.4 us -> 59.5 us  [the longest x1 54.6 us: per_device(): pl.pallas_call(functools.partial(correlate_kernel, tiles, days, group, no...]
where the time goes in v3:
time: 66.4 us; the launch traced here: 66.1 us
  Pallas kernels  59.5 us (90%)
  local copies, waits for them, and re-layouts  6.56 us (10%)
    pallas_call x1, Pallas kernels, per_device(): pl.pallas_call(functools.partial(correlate_kernel, tiles, days, group, no...  54.6 us
    unnamed x3, local copies, waits for them, and re-layouts  6.56 us
    pallas_call x1, Pallas kernels, per_device(): pl.pallas_call(whiten_kernel, grid=(segments,), out_shape=[jax.ShapeDtype...  4.95 us

profile of v3, /device:TPU:14, one launch (start us, length us, event | category | flops | bytes accessed | tf_op | source)
XLA Modules:
  0.0 66.1 jit_solution(17373537754449593282)
XLA Ops:
  0.0 1.3 %copy.7.pair_ref = s32[4,2]{1,0:T(4,128)} copy(s32[4,2]{0,1:T(2,128)} %param.8) | data formatting | bytes 64 | tf_op args[3]
  1.3 3.6 %copy.6 = bf16[1,256,2,4,512]{4,1,2,3,0:T(8,128)(2,1)} copy(bf16[1,256,2,4,512]{4,3,2,1,0:T(4,128)(2,1)} %param.5) | data formatting | bytes 4194304 | tf_op args[0]
  4.9 5.0 %shard_map.55 = (bf16[4,2,2,128,512]{4,3,2,1,0:T(8,128)(2,1)}, s32[8,128]{1,0:T(8,128)}) custom-call(s32[2]{0:T(128)} %low_ref.1, s32[2]{0:T(128)} %high_ref.1, s32[4,2]{1,0:T(4,128)} %copy.7.pair_ref, bf16[4,2,2,128,512]{4,3,2,1,0:T(8,128)(2,1)} %bitcast.3), custom_call_target="tpu_custom_call" | custom-call | tf_op jit(solution)/shard_map/pallas_call | solution.py:410
  9.8 54.6 %shard_map.56 = f32[1,4,128,128]{3,2,1,0:T(8,128)} custom-call(s32[8,128]{1,0:T(8,128)} %get-tuple-element.7.own_pair_ref, f32[2,2,512]{2,1,0:T(2,128)} %constant.2.clone.trig_ref, bf16[4,2,2,128,512]{4,3,2,1,0:T(8,128)(2,1)} %get-tuple-element.8.own_ref), custom_call_target="tpu_custom_call" | custom-call | tf_op jit(solution)/shard_map/pallas_call | solution.py:428
  64.4 1.7 %copy.9 = f32[1,4,128,128]{3,2,1,0:T(8,128)} copy(f32[1,4,128,128]{3,2,1,0:T(8,128)} %shard_map.56) | data formatting | bytes 524288

commit v4 on v3

--- a/solution.py
+++ b/solution.py
@@ -39,46 +39,9 @@
     return result
 
 
-def whiten_kernel(low_ref, high_ref, pair_ref, raw_ref, out_ref, padded_ref, spread_ref):
-    bins = raw_ref.shape[-1]
-
-    @pl.when(pl.program_id(0) == 0)
-    def _():
-        row = lax.broadcasted_iota(jnp.int32, (bins, bins), 0)
-        col = lax.broadcasted_iota(jnp.int32, (bins, bins), 1)
-        spread_ref[...] = jnp.where(jnp.abs(row - col) <= HALF_WIN, 1.0, 0.0).astype(jnp.bfloat16)
-        row = lax.broadcasted_iota(jnp.int32, padded_ref.shape, 0)
-        col = lax.broadcasted_iota(jnp.int32, padded_ref.shape, 1)
-        padded = jnp.full(padded_ref.shape, -1, jnp.int32)
-        for pair in range(pair_ref.shape[0]):
-            for side in range(2):
-                padded = jnp.where((row == pair) & (col == side), pair_ref[pair, side], padded)
-        padded_ref[...] = padded
-
-    bin_index = lax.broadcasted_iota(jnp.int32, (1, bins), 1)
-    counts = (
-        jnp.minimum(bin_index + HALF_WIN, bins - 1) - jnp.maximum(bin_index - HALF_WIN, 0) + 1
-    ).astype(jnp.float32)
-    spread = spread_ref[...]
-    for block in range(BLK_DEV):
-        real = raw_ref[0, 0, block].astype(jnp.float32)
-        imag = raw_ref[0, 1, block].astype(jnp.float32)
-        magnitude = jnp.sqrt(real * real + imag * imag)
-        coarse = magnitude.astype(jnp.bfloat16)
-        fine = (magnitude - coarse.astype(jnp.float32)).astype(jnp.bfloat16)
-        sums = jnp.dot(coarse, spread, preferred_element_type=jnp.float32) + jnp.dot(
-            fine, spread, preferred_element_type=jnp.float32
-        )
-        amplitude = sums / counts + 1e-05
-        keep = (bin_index >= low_ref[block]) & (bin_index < high_ref[block])
-        gain = 1.0 / amplitude
-        out_ref[0, 0, block] = jnp.where(keep, real * gain, 0.0).astype(jnp.bfloat16)
-        out_ref[0, 1, block] = jnp.where(keep, imag * gain, 0.0).astype(jnp.bfloat16)
-
-
 def correlate_kernel(
-    tiles, days, group, norm_factor, own_pair_ref, trig_ref, own_ref, out_ref,
-    win_ref, gath_ref, pair_ref,
+    tiles, days, group, norm_factor, low_ref, high_ref, own_pair_ref, trig_ref, raw_ref, out_ref,
+    own_ref, spread_ref, win_ref, gath_ref, pair_ref,
     rot_ref, part_ref, day_buf, send_buf, recv_buf, top_buf, down_src, down_buf,
     send_sem, recv_sem, far_send, far_recv, pair_send, pair_recv, up_send, up_recv, own_sem,
     day_send, day_recv, tile_send, tile_recv, top_send, top_recv, down_send, down_recv,
@@ -117,8 +80,38 @@
     def _():
         pl.semaphore_signal(barrier, inc=1, device_id={"tile": here + group}, device_id_type=MESH)
 
+    bins = raw_ref.shape[-1]
+    row = lax.broadcasted_iota(jnp.int32, (bins, bins), 0)
+    col = lax.broadcasted_iota(jnp.int32, (bins, bins), 1)
+    spread_ref[...] = jnp.where(jnp.abs(row - col) <= HALF_WIN, 1.0, 0.0).astype(jnp.bfloat16)
+    bin_index = lax.broadcasted_iota(jnp.int32, (1, bins), 1)
+    counts = (
+        jnp.minimum(bin_index + HALF_WIN, bins - 1) - jnp.maximum(bin_index - HALF_WIN, 0) + 1
+    ).astype(jnp.float32)
+    gath_ref[BELOW + spot, 0:rows_dev, 0:2] = own_pair_ref[...]
+
+    @pl.when(base == 0)
+    def _():
+        gath_ref[0] = jnp.full(gath_ref.shape[1:], -1, jnp.int32)
+
     peers = days - 1 + group - 1 + has_below.astype(jnp.int32) + has_above.astype(jnp.int32)
     pl.semaphore_wait(barrier, peers)
+
+    def whiten(there, block):
+        real = raw_ref[there, 0, block].astype(jnp.float32)
+        imag = raw_ref[there, 1, block].astype(jnp.float32)
+        magnitude = jnp.sqrt(real * real + imag * imag)
+        coarse = magnitude.astype(jnp.bfloat16)
+        fine = (magnitude - coarse.astype(jnp.float32)).astype(jnp.bfloat16)
+        spread = spread_ref[...]
+        sums = jnp.dot(coarse, spread, preferred_element_type=jnp.float32) + jnp.dot(
+            fine, spread, preferred_element_type=jnp.float32
+        )
+        amplitude = sums / counts + 1e-05
+        keep = (bin_index >= low_ref[block]) & (bin_index < high_ref[block])
+        gain = 1.0 / amplitude
+        own_ref[there, 0, block] = jnp.where(keep, real * gain, 0.0).astype(jnp.bfloat16)
+        own_ref[there, 1, block] = jnp.where(keep, imag * gain, 0.0).astype(jnp.bfloat16)
 
     def across(offset, chunk):
         block, part = divmod(chunk, 2)
@@ -134,7 +127,7 @@
 
     def pairs_across(offset):
         return pltpu.make_async_remote_copy(
-            src_ref=own_pair_ref,
+            src_ref=gath_ref.at[BELOW + spot],
             dst_ref=gath_ref.at[BELOW + spot],
             send_sem=pair_send.at[offset - 1],
             recv_sem=pair_recv.at[offset - 1],
@@ -177,19 +170,25 @@
             for chunk in chunk_list:
                 far(source, slot, 0, here + group, chunk).start()
 
-    for offset in range(1, group):
-        pairs_across(offset).start()
-    for chunk in range(chunks):
-        for offset in range(1, group):
-            across(offset, chunk).start()
-    relay(own_ref, spot, spot, range(chunks))
+    def send(offset, block):
+        if offset:
+            for part in range(2):
+                across(offset, 2 * block + part).start()
+        else:
+            relay(own_ref, spot, spot, [2 * block, 2 * block + 1])
+
+    turns = list(range(1, last)) + [0, last]
+    items = [(offset, block) for block in range(BLK_DEV) for offset in turns]
+    for index, (offset, block) in enumerate(items):
+        whiten(mixed(spot, offset), block)
+        if index:
+            send(*items[index - 1])
+        else:
+            for peer in range(1, group):
+                pairs_across(peer).start()
+    send(*items[-1])
     stay = pltpu.make_async_copy(own_ref.at[spot], win_ref.at[BELOW + spot], own_sem)
     stay.start()
-    gath_ref[BELOW + spot] = own_pair_ref[...]
-
-    @pl.when(base == 0)
-    def _():
-        gath_ref[0] = jnp.full(own_pair_ref.shape, -1, jnp.int32)
 
     for chunk in range(chunks):
         for offset in range(1, group):
@@ -284,19 +283,19 @@
             total = total + day_buf[step - 1, slot]
         return total
 
-    def tile_copy(offset):
-        return pltpu.make_async_remote_copy(
-            src_ref=send_buf.at[offset - 1],
-            dst_ref=recv_buf.at[offset - 1],
-            send_sem=tile_send.at[offset - 1],
-            recv_sem=tile_recv.at[offset - 1],
-            device_id={"tile": base + mixed(spot, offset)},
+    def tile_copy(target, source):
+        return pltpu.make_async_remote_copy(
+            src_ref=send_buf.at[target],
+            dst_ref=recv_buf.at[source],
+            send_sem=tile_send.at[target],
+            recv_sem=tile_recv.at[source],
+            device_id={"tile": base + target},
             device_id_type=MESH,
         )
 
     def top_copy(device, slot):
         return pltpu.make_async_remote_copy(
-            src_ref=send_buf.at[last],
+            src_ref=send_buf.at[group],
             dst_ref=top_buf.at[slot],
             send_sem=top_send,
             recv_sem=top_recv.at[slot],
@@ -314,16 +313,29 @@
             device_id_type=MESH,
         )
 
-    def push(offset):
-        send_buf[offset - 1] = day_total(offset).astype(jnp.bfloat16)
-        tile_copy(offset).start()
-
-    for offset in range(last, -1, -1):
-        products((mixed(spot, offset) + BELOW) % group, offset)
+    def destination(step):
+        return (spot + step) % last if step else jnp.int32(last)
+
+    def push(step):
+        target = destination(step)
+        total = day_total(target)
+
+        @pl.when(target == spot)
+        def _():
+            out_ref[0] = total
+
+        @pl.when(target != spot)
+        def _():
+            send_buf[target] = total.astype(jnp.bfloat16)
+            tile_copy(target, spot).start()
+
+    for turn in range(group):
+        target = destination(turn)
+        products((target + BELOW) % group, target)
         for step in range(1, days):
-            day_copy(step, offset).start()
-        if offset < last:
-            push(offset + 1)
+            day_copy(step, target).start()
+        if turn:
+            push(turn - 1)
 
     @pl.when(is_top)
     def _():
@@ -331,7 +343,7 @@
         for step in range(1, days):
             day_copy(step, group).start()
 
-    out_ref[0] = day_total(0)
+    push(last)
 
     @pl.when(is_top)
     def _():
@@ -339,37 +351,37 @@
 
         @pl.when(spot < last)
         def _():
-            send_buf[last] = total.astype(jnp.bfloat16)
+            send_buf[group] = total.astype(jnp.bfloat16)
             top_copy(base + last, spot).start()
 
         @pl.when(spot == last)
         def _():
-            down_buf[...] = total
+            part_ref[group, day] = total
 
     for offset in range(last, 0, -1):
-        tile_copy(offset).wait_recv()
+        tile_copy(spot, mixed(spot, offset)).wait_recv()
     sends_down = has_below & (spot == last)
     takes_down = has_above & (spot == last)
     for row in range(rows_dev):
         total = out_ref[0, row]
         for offset in range(last, 0, -1):
-            total = total + recv_buf[offset - 1, row].astype(jnp.float32)
+            total = total + recv_buf[mixed(spot, offset), row].astype(jnp.float32)
         out_ref[0, row] = total
 
         @pl.when(sends_down)
         def _():
-            down_src[row] = total
+            down_src[row] = total.astype(jnp.bfloat16)
             down_copy(row, here - group).start()
 
     @pl.when(takes_down)
     def _():
         for row in range(rows_dev):
             down_copy(row, here).wait_recv()
-            out_ref[0, row] = down_buf[row]
+            out_ref[0, row] = down_buf[row].astype(jnp.float32)
 
     @pl.when(is_top & (spot == last))
     def _():
-        total = down_buf[...]
+        total = part_ref[group, day]
         for slot in range(last):
             top_copy(here, slot).wait_recv()
             total = total + top_buf[slot].astype(jnp.float32)
@@ -385,7 +397,7 @@
             down_copy(row, here - group).wait_send()
 
     for offset in range(last, 0, -1):
-        tile_copy(offset).wait_send()
+        tile_copy(mixed(spot, offset), spot).wait_send()
     for offset in range(last, -1, -1):
         for step in range(1, days):
             day_copy(step, offset).wait_send()
@@ -407,41 +419,28 @@
     slice_shape = (parts, BLK_DEV, chans, bins)
     raw = jnp.transpose(own.reshape(BLK_DEV, chans, parts, segments, bins), (3, 2, 0, 1, 4))
 
-    whitened, padded = pl.pallas_call(
-        whiten_kernel,
-        grid=(segments,),
-        out_shape=[
-            jax.ShapeDtypeStruct((segments,) + slice_shape, jnp.bfloat16),
-            jax.ShapeDtypeStruct((8, 128), jnp.int32),
-        ],
-        in_specs=[SMEM, SMEM, SMEM, pl.BlockSpec((1,) + slice_shape, lambda s: (s, 0, 0, 0, 0))],
-        out_specs=[
-            pl.BlockSpec((1,) + slice_shape, lambda s: (s, 0, 0, 0, 0)),
-            pl.BlockSpec((8, 128), lambda s: (0, 0)),
-        ],
-        scratch_shapes=[pltpu.VMEM((bins, bins), jnp.bfloat16)],
-    )(band_low, band_high, pair_list, raw)
-
     chunks = 2 * BLK_DEV
     block_shape = (rows_dev, chans, chans)
     gathered_shape = (BELOW + group, 8, 128)
     return pl.pallas_call(
         functools.partial(correlate_kernel, tiles, days, group, norm_factor),
         out_shape=jax.ShapeDtypeStruct((1,) + block_shape, jnp.float32),
-        in_specs=[VMEM, VMEM, VMEM],
+        in_specs=[SMEM, SMEM, VMEM, VMEM, VMEM],
         out_specs=VMEM,
         scratch_shapes=[
+            pltpu.VMEM((segments,) + slice_shape, jnp.bfloat16),
+            pltpu.VMEM((bins, bins), jnp.bfloat16),
             pltpu.VMEM((group + REACH,) + slice_shape, jnp.bfloat16),
             pltpu.VMEM(gathered_shape, jnp.int32),
             pltpu.SMEM(gathered_shape, jnp.int32),
             pltpu.VMEM(((group + REACH) * BLK_DEV, parts, lags * chans, bins), jnp.bfloat16),
             pltpu.VMEM((group + 1, lags) + block_shape, jnp.float32),
             pltpu.VMEM((days - 1, group + 1) + block_shape, jnp.float32),
+            pltpu.VMEM((group + 1,) + block_shape, jnp.bfloat16),
             pltpu.VMEM((group,) + block_shape, jnp.bfloat16),
             pltpu.VMEM((group - 1,) + block_shape, jnp.bfloat16),
-            pltpu.VMEM((group - 1,) + block_shape, jnp.bfloat16),
-            pltpu.VMEM(block_shape, jnp.float32),
-            pltpu.VMEM(block_shape, jnp.float32),
+            pltpu.VMEM(block_shape, jnp.bfloat16),
+            pltpu.VMEM(block_shape, jnp.bfloat16),
             pltpu.SemaphoreType.DMA((group - 1, chunks)),
             pltpu.SemaphoreType.DMA((group - 1, chunks)),
             pltpu.SemaphoreType.DMA((REACH, chunks)),
@@ -453,8 +452,8 @@
             pltpu.SemaphoreType.DMA,
             pltpu.SemaphoreType.DMA((days - 1, group + 1)),
             pltpu.SemaphoreType.DMA((days - 1, group + 1)),
-            pltpu.SemaphoreType.DMA((group - 1,)),
-            pltpu.SemaphoreType.DMA((group - 1,)),
+            pltpu.SemaphoreType.DMA((group,)),
+            pltpu.SemaphoreType.DMA((group,)),
             pltpu.SemaphoreType.DMA,
             pltpu.SemaphoreType.DMA((group - 1,)),
             pltpu.SemaphoreType.DMA((rows_dev,)),
@@ -463,7 +462,7 @@
         compiler_params=pltpu.CompilerParams(
             collective_id=0, has_side_effects=True, vmem_limit_bytes=63 * 1024 * 1024
         ),
-    )(padded, jnp.asarray(phase_tables(lags, bins)), whitened)
+    )(band_low, band_high, pair_list, jnp.asarray(phase_tables(lags, bins)), raw)
 
 
 def solution(mesh):

time: 66.4 us -> 59.4 us (0.89)
  the two profiles are of different devices: /device:TPU:14 before, /device:TPU:0 now
where the time goes in v4:
time: 59.4 us; the launch traced here: 59.2 us
  Pallas kernels  52.6 us (89%)
  local copies, waits for them, and re-layouts  6.61 us (11%)
    pallas_call x1, Pallas kernels, per_device(): pl.pallas_call(functools.partial(correlate_kernel, tiles, days, group, no...  52.6 us
    unnamed x3, local copies, waits for them, and re-layouts  6.61 us

profile of v4, /device:TPU:0, one launch (start us, length us, event | category | flops | bytes accessed | tf_op | source)
XLA Modules:
  0.0 59.2 jit_solution(4447523225834436299)
XLA Ops:
  0.0 1.3 %copy.7.own_pair_ref = s32[4,2]{1,0:T(4,128)} copy(s32[4,2]{0,1:T(2,128)} %param.8) | data formatting | bytes 64 | tf_op args[3]
  1.3 3.6 %copy.6 = bf16[1,256,2,4,512]{4,1,2,3,0:T(8,128)(2,1)} copy(bf16[1,256,2,4,512]{4,3,2,1,0:T(4,128)(2,1)} %param.5) | data formatting | bytes 4194304 | tf_op args[0]
  4.9 52.6 %shard_map.55 = f32[1,4,128,128]{3,2,1,0:T(8,128)} custom-call(s32[2]{0:T(128)} %low_ref.1, s32[2]{0:T(128)} %high_ref.1, s32[4,2]{1,0:T(4,128)} %copy.7.own_pair_ref, f32[2,2,512]{2,1,0:T(2,128)} %constant.2.clone.trig_ref, bf16[4,2,2,128,512]{4,3,2,1,0:T(8,128)(2,1)} %bitcast.3), custom_call_target="tpu_custom_call" | custom-call | tf_op jit(solution)/shard_map/pallas_call | solution.py:425
  57.5 1.7 %copy.9 = f32[1,4,128,128]{3,2,1,0:T(8,128)} copy(f32[1,4,128,128]{3,2,1,0:T(8,128)} %shard_map.55) | data formatting | bytes 524288

commit v5 on v4

--- a/solution.py
+++ b/solution.py
@@ -88,7 +88,7 @@
     counts = (
         jnp.minimum(bin_index + HALF_WIN, bins - 1) - jnp.maximum(bin_index - HALF_WIN, 0) + 1
     ).astype(jnp.float32)
-    gath_ref[BELOW + spot, 0:rows_dev, 0:2] = own_pair_ref[...]
+    gath_ref[BELOW + spot, 0:2, 0:rows_dev] = own_pair_ref[...]
 
     @pl.when(base == 0)
     def _():
@@ -249,8 +249,8 @@
 
     def products(set_index, slot):
         for row in range(rows_dev):
-            first = pair_ref[set_index, row, 0]
-            second = pair_ref[set_index, row, 1]
+            first = pair_ref[set_index, 0, row]
+            second = pair_ref[set_index, 1, row]
             left = jnp.clip(first - base_block, 0, window_tiles * BLK_DEV - 1)
             right = jnp.clip(second - base_block, 0, window_tiles * BLK_DEV - 1)
             total = jnp.zeros((chans, lags * chans), jnp.float32)
@@ -314,7 +314,8 @@
         )
 
     def destination(step):
-        return (spot + step) % last if step else jnp.int32(last)
+        is_last = spot // last
+        return is_last * step + (1 - is_last) * ((spot + step) % last if step else last)
 
     def push(step):
         target = destination(step)
@@ -462,7 +463,7 @@
         compiler_params=pltpu.CompilerParams(
             collective_id=0, has_side_effects=True, vmem_limit_bytes=63 * 1024 * 1024
         ),
-    )(band_low, band_high, pair_list, jnp.asarray(phase_tables(lags, bins)), raw)
+    )(band_low, band_high, pair_list.T, jnp.asarray(phase_tables(lags, bins)), raw)
 
 
 def solution(mesh):

time: 59.4 us -> 56.3 us (0.948)
  Pallas kernels: 52.6 us -> 50.8 us
  local copies, waits for them, and re-layouts: 6.61 us -> 5.27 us
    pallas_call x1, Pallas kernels: 52.6 us -> 50.8 us  [per_device(): pl.pallas_call(functools.partial(correlate_kernel, tiles, days, group, no...]
    unnamed x3 -> x2, local copies, waits for them, and re-layouts: 6.61 us -> 5.27 us
where the time goes in v5:
time: 56.3 us; the launch traced here: 56.1 us
  Pallas kernels  50.8 us (90%)
  local copies, waits for them, and re-layouts  5.27 us (9%)
    pallas_call x1, Pallas kernels, per_device(): pl.pallas_call(functools.partial(correlate_kernel, tiles, days, group, no...  50.8 us
    unnamed x2, local copies, waits for them, and re-layouts  5.27 us

profile of v5, /device:TPU:0, one launch (start us, length us, event | category | flops | bytes accessed | tf_op | source)
XLA Modules:
  0.0 56.1 jit_solution(9321442973132439613)
XLA Ops:
  0.0 3.6 %copy.6 = bf16[1,256,2,4,512]{4,1,2,3,0:T(8,128)(2,1)} copy(bf16[1,256,2,4,512]{4,3,2,1,0:T(4,128)(2,1)} %param.5) | data formatting | bytes 4194304 | tf_op args[0]
  3.6 50.8 %shard_map.55 = f32[1,4,128,128]{3,2,1,0:T(8,128)} custom-call(s32[2]{0:T(128)} %low_ref.1, s32[2]{0:T(128)} %high_ref.1, s32[2,4]{1,0:T(2,128)} %bitcast.5, f32[2,2,512]{2,1,0:T(2,128)} %constant.2.clone.trig_ref, bf16[4,2,2,128,512]{4,3,2,1,0:T(8,128)(2,1)} %bitcast.4), custom_call_target="tpu_custom_call" | custom-call | tf_op jit(solution)/shard_map/pallas_call | solution.py:426
  54.4 1.7 %copy.8 = f32[1,4,128,128]{3,2,1,0:T(8,128)} copy(f32[1,4,128,128]{3,2,1,0:T(8,128)} %shard_map.55) | data formatting | bytes 524288

commit v6 on v5

--- a/solution.py
+++ b/solution.py
@@ -40,8 +40,8 @@
 
 
 def correlate_kernel(
-    tiles, days, group, norm_factor, low_ref, high_ref, own_pair_ref, trig_ref, raw_ref, out_ref,
-    own_ref, spread_ref, win_ref, gath_ref, pair_ref,
+    tiles, days, group, norm_factor, low_ref, high_ref, own_pair_ref, trig_ref, raw_hbm, out_ref,
+    raw_ref, raw_sem, own_ref, spread_ref, win_ref, gath_ref, pair_ref,
     rot_ref, part_ref, day_buf, send_buf, recv_buf, top_buf, down_src, down_buf,
     send_sem, recv_sem, far_send, far_recv, pair_send, pair_recv, up_send, up_recv, own_sem,
     day_send, day_recv, tile_send, tile_recv, top_send, top_recv, down_send, down_recv,
@@ -56,6 +56,17 @@
     upper = REACH - BELOW
 
     last = group - 1
+    turns = list(range(1, last)) + [0, last]
+    items = [(offset, block) for block in range(BLK_DEV) for offset in turns]
+
+    def fetch(offset, block):
+        there = mixed(spot, offset)
+        return pltpu.make_async_copy(
+            raw_hbm.at[there, :, block], raw_ref.at[there, :, block], raw_sem.at[offset, block]
+        )
+
+    for item in items:
+        fetch(*item).start()
     is_top = base + group == tiles
     base_block = (base - BELOW) * BLK_DEV
     window_tiles, _, _, chans, _ = win_ref.shape
@@ -177,9 +188,8 @@
         else:
             relay(own_ref, spot, spot, [2 * block, 2 * block + 1])
 
-    turns = list(range(1, last)) + [0, last]
-    items = [(offset, block) for block in range(BLK_DEV) for offset in turns]
     for index, (offset, block) in enumerate(items):
+        fetch(offset, block).wait()
         whiten(mixed(spot, offset), block)
         if index:
             send(*items[index - 1])
@@ -426,9 +436,11 @@
     return pl.pallas_call(
         functools.partial(correlate_kernel, tiles, days, group, norm_factor),
         out_shape=jax.ShapeDtypeStruct((1,) + block_shape, jnp.float32),
-        in_specs=[SMEM, SMEM, VMEM, VMEM, VMEM],
+        in_specs=[SMEM, SMEM, VMEM, VMEM, pl.BlockSpec(memory_space=pl.ANY)],
         out_specs=VMEM,
         scratch_shapes=[
+            pltpu.VMEM((segments,) + slice_shape, jnp.bfloat16),
+            pltpu.SemaphoreType.DMA((group, BLK_DEV)),
             pltpu.VMEM((segments,) + slice_shape, jnp.bfloat16),
             pltpu.VMEM((bins, bins), jnp.bfloat16),
             pltpu.VMEM((group + REACH,) + slice_shape, jnp.bfloat16),

time: 56.3 us -> 55.5 us (0.986)
  Pallas kernels: 50.8 us -> 50 us
    pallas_call x1, Pallas kernels: 50.8 us -> 50 us  [per_device(): pl.pallas_call(functools.partial(correlate_kernel, tiles, days, group, no...]
where the time goes in v6:
time: 55.5 us; the launch traced here: 55.3 us
  Pallas kernels  50 us (90%)
  local copies, waits for them, and re-layouts  5.27 us (9%)
    pallas_call x1, Pallas kernels, per_device(): pl.pallas_call(functools.partial(correlate_kernel, tiles, days, group, no...  50 us
    unnamed x2, local copies, waits for them, and re-layouts  5.27 us

profile of v6, /device:TPU:0, one launch (start us, length us, event | category | flops | bytes accessed | tf_op | source)
XLA Modules:
  0.0 55.3 jit_solution(3404615980867184723)
XLA Ops:
  0.0 3.6 %copy.6 = bf16[1,256,2,4,512]{4,1,2,3,0:T(8,128)(2,1)} copy(bf16[1,256,2,4,512]{4,3,2,1,0:T(4,128)(2,1)} %param.5) | data formatting | bytes 4194304 | tf_op args[0]
  3.6 50.0 %shard_map.55 = f32[1,4,128,128]{3,2,1,0:T(8,128)} custom-call(s32[2]{0:T(128)} %low_ref.1, s32[2]{0:T(128)} %high_ref.1, s32[2,4]{1,0:T(2,128)} %bitcast.5, f32[2,2,512]{2,1,0:T(2,128)} %constant.2.clone.trig_ref, bf16[4,2,2,128,512]{4,3,2,1,0:T(8,128)(2,1)} %bitcast.4), custom_call_target="tpu_custom_call" | custom-call | tf_op jit(solution)/shard_map/pallas_call | solution.py:436
  53.6 1.7 %copy.8 = f32[1,4,128,128]{3,2,1,0:T(8,128)} copy(f32[1,4,128,128]{3,2,1,0:T(8,128)} %shard_map.55) | data formatting | bytes 524288
